TPU v7x, 128 devices: a whole 4x4x4 slice. The times are simulated.
128 devices in a mesh: dp: 8 (over z, core), et: 16 (over y, x).
Axes of the slice: x: 4, y: 4, z: 4, core: 2. Of those that a mesh axis runs over, the one named last changes fastest.
Arguments:
- routed_rows: bfloat16 [4096, 4096], P(('dp', 'et')), may hold values from -6 to 6
- out_cotangent: bfloat16 [4096, 4096], P(('dp', 'et')), may hold values from -6 to 6
- route_weight: float32 [4096], P(('dp', 'et')), may hold values from 0.1 to 1
- expert_counts: int32 [8, 2], replicated, may hold values from 1 to 256, as said below
- w_gate: bfloat16 [2, 4096, 7168], P(None, None, 'et'), may hold values from -0.09375 to 0.09375
- w_up: bfloat16 [2, 4096, 7168], P(None, None, 'et'), may hold values from -0.09375 to 0.09375
- w_down: bfloat16 [2, 7168, 4096], P(None, 'et'), may hold values from -0.0625 to 0.0625
Outputs:
- layer_out: bfloat16 [4096, 4096], P(('dp', 'et'))
- grad_weight: float32 [4096], P(('dp', 'et'))
- grad_rows: bfloat16 [4096, 4096], P(('dp', 'et'))
- grad_gate: bfloat16 [2, 4096, 7168], P(None, 'dp', 'et')
- grad_up: bfloat16 [2, 4096, 7168], P(None, 'dp', 'et')
- grad_down: bfloat16 [2, 7168, 4096], P(None, 'et', 'dp')
Inputs may be any that keep to these rules, and one draw needn't show every extreme that they name: `expert_counts`: both counts of a group, each rounded up to a multiple of 128, sum to at most 512; in some group both counts equal 256.
All inputs are finite; a program needn't handle non-finite values.
Results may differ from a plain program's by a relative error of at most 0.029.
Values may be sent and summed in bfloat16 or wider, within the bound.
A program may use at most 192 MiB of HBM per device.

v0:
```python
import jax
import jax.numpy as jnp
from jax import lax
from jax.sharding import PartitionSpec as P

BLOCK = 128


def block_layout(counts_row, block_rows, slot_count):
    padded = (counts_row + block_rows - 1) // block_rows * block_rows
    starts = jnp.cumsum(padded) - padded
    position = jnp.arange(slot_count, dtype=jnp.int32)
    relative = position[:, None] - starts[None, :]
    live_rows = jnp.any((relative >= 0) & (relative < counts_row[None, :]), axis=1)
    block_first = jnp.arange(slot_count // block_rows, dtype=jnp.int32) * block_rows
    block_rel = block_first[:, None] - starts[None, :]
    owned = (block_rel >= 0) & (block_rel < padded[None, :])
    expert_ids = jnp.arange(counts_row.shape[0], dtype=jnp.int32)
    block_expert = jnp.sum(jnp.where(owned, expert_ids[None, :], 0), axis=1)
    live_blocks = jnp.sum(padded) // block_rows
    return (live_rows, block_expert, live_blocks)


def contract_rows(left, right):
    return lax.dot_general(
        left, right, (((0,), (0,)), ((), ())), preferred_element_type=jnp.float32
    )


def contract_cols(left, right):
    return lax.dot_general(
        left, right, (((1,), (1,)), ((), ())), preferred_element_type=jnp.float32
    )


def per_device(routed_rows, out_cotangent, route_weight, expert_counts, w_gate, w_up, w_down):
    row_dev = routed_rows.shape[0]
    model_width = routed_rows.shape[1]
    hidden_width = w_gate.shape[2]
    slot_count = row_dev * lax.axis_size("et")
    block_rows = BLOCK
    block_count = slot_count // block_rows
    group_index = lax.axis_index("dp")
    live_rows, block_expert, live_blocks = block_layout(
        expert_counts[group_index], block_rows, slot_count
    )
    row_mask = live_rows[:, None]
    gathered = lax.all_gather(routed_rows, "et", axis=0, tiled=True)

    def forward_step(step, loop_state):
        gate_all, lin_all, hidden_all, share_all = loop_state
        row_start = step * block_rows
        expert = block_expert[step]
        row_block = lax.dynamic_slice_in_dim(gathered, row_start, block_rows, 0)
        mask_block = lax.dynamic_slice_in_dim(row_mask, row_start, block_rows, 0)
        gate_pre = jnp.dot(row_block, w_gate[expert], preferred_element_type=jnp.float32)
        lin_pre = jnp.dot(row_block, w_up[expert], preferred_element_type=jnp.float32)
        hidden = jnp.where(mask_block, jax.nn.silu(gate_pre) * lin_pre, 0.0).astype(jnp.bfloat16)
        share_term = jnp.dot(hidden, w_down[expert], preferred_element_type=jnp.float32)
        return (
            lax.dynamic_update_slice_in_dim(gate_all, gate_pre, row_start, 0),
            lax.dynamic_update_slice_in_dim(lin_all, lin_pre, row_start, 0),
            lax.dynamic_update_slice_in_dim(hidden_all, hidden, row_start, 0),
            lax.dynamic_update_slice_in_dim(share_all, share_term, row_start, 0),
        )

    forward_init = (
        jnp.zeros((slot_count, hidden_width), jnp.float32),
        jnp.zeros((slot_count, hidden_width), jnp.float32),
        jnp.zeros((slot_count, hidden_width), jnp.bfloat16),
        jnp.zeros((slot_count, model_width), jnp.float32),
    )
    gate_all, lin_all, hidden_all, share_all = lax.fori_loop(
        0, block_count, forward_step, forward_init
    )
    combined = lax.psum_scatter(
        share_all.astype(jnp.bfloat16), "et", scatter_dimension=0, tiled=True
    ).astype(jnp.float32)
    layer_out = (route_weight[:, None] * combined).astype(jnp.bfloat16)
    grad_weight = jnp.sum(out_cotangent.astype(jnp.float32) * combined, axis=1)
    scaled_local = (route_weight[:, None] * out_cotangent.astype(jnp.float32)).astype(jnp.bfloat16)
    scaled = lax.all_gather(scaled_local, "et", axis=0, tiled=True)

    def backward_step(step, loop_state):
        grad_gate_all, grad_lin_all, rows_all = (loop_state[0], loop_state[1], loop_state[2])
        row_start = step * block_rows
        expert = block_expert[step]
        scaled_block = lax.dynamic_slice_in_dim(scaled, row_start, block_rows, 0)
        gate_block = lax.dynamic_slice_in_dim(gate_all, row_start, block_rows, 0)
        lin_block = lax.dynamic_slice_in_dim(lin_all, row_start, block_rows, 0)
        mask_block = lax.dynamic_slice_in_dim(row_mask, row_start, block_rows, 0)
        grad_hidden = contract_cols(scaled_block, w_down[expert])
        logistic = jax.nn.sigmoid(gate_block)
        grad_gate_pre = jnp.where(
            mask_block,
            grad_hidden * lin_block * logistic * (1.0 + gate_block * (1.0 - logistic)),
            0.0,
        ).astype(jnp.bfloat16)
        grad_lin_pre = jnp.where(mask_block, grad_hidden * gate_block * logistic, 0.0).astype(
            jnp.bfloat16
        )
        rows_term = contract_cols(grad_gate_pre, w_gate[expert]) + contract_cols(
            grad_lin_pre, w_up[expert]
        )
        updated = (
            lax.dynamic_update_slice_in_dim(grad_gate_all, grad_gate_pre, row_start, 0),
            lax.dynamic_update_slice_in_dim(grad_lin_all, grad_lin_pre, row_start, 0),
            lax.dynamic_update_slice_in_dim(rows_all, rows_term, row_start, 0),
        )
        row_block = lax.dynamic_slice_in_dim(gathered, row_start, block_rows, 0)
        hidden_block = lax.dynamic_slice_in_dim(hidden_all, row_start, block_rows, 0)
        updated = updated + (
            loop_state[3].at[expert].add(contract_rows(row_block, grad_gate_pre)),
            loop_state[4].at[expert].add(contract_rows(row_block, grad_lin_pre)),
            loop_state[5].at[expert].add(contract_rows(hidden_block, scaled_block)),
        )
        return updated

    backward_init = (
        jnp.zeros((slot_count, hidden_width), jnp.bfloat16),
        jnp.zeros((slot_count, hidden_width), jnp.bfloat16),
        jnp.zeros((slot_count, model_width), jnp.float32),
    )
    backward_init = backward_init + (
        jnp.zeros(w_gate.shape, jnp.float32),
        jnp.zeros(w_up.shape, jnp.float32),
        jnp.zeros(w_down.shape, jnp.float32),
    )
    backward = lax.fori_loop(0, block_count, backward_step, backward_init)
    grad_gate_all, grad_lin_all, rows_all = (backward[0], backward[1], backward[2])
    grad_rows = lax.psum_scatter(
        rows_all.astype(jnp.bfloat16), "et", scatter_dimension=0, tiled=True
    )
    summed = (
        lax.psum_scatter(
            backward[3].astype(jnp.bfloat16), "dp", scatter_dimension=1, tiled=True
        ).astype(jnp.float32),
        lax.psum_scatter(
            backward[4].astype(jnp.bfloat16), "dp", scatter_dimension=1, tiled=True
        ).astype(jnp.float32),
        lax.psum_scatter(
            backward[5].astype(jnp.bfloat16), "dp", scatter_dimension=2, tiled=True
        ).astype(jnp.float32),
    )
    grad_gate = summed[0].astype(jnp.bfloat16)
    grad_up = summed[1].astype(jnp.bfloat16)
    grad_down = summed[2].astype(jnp.bfloat16)
    return (layer_out, grad_weight, grad_rows, grad_gate, grad_up, grad_down)


def solution(mesh):
    return jax.shard_map(
        per_device,
        mesh=mesh,
        in_specs=(
            P(("dp", "et"), None),
            P(("dp", "et"), None),
            P(("dp", "et")),
            P(),
            P(None, None, "et"),
            P(None, None, "et"),
            P(None, "et", None),
        ),
        out_specs=(
            P(("dp", "et"), None),
            P(("dp", "et")),
            P(("dp", "et"), None),
            P(None, "dp", "et"),
            P(None, "dp", "et"),
            P(None, "et", "dp"),
        ),
        check_vma=False,
    )
```

profile of v0, /device:TPU:1, one launch (start us, length us, event | category | flops | bytes accessed | tf_op | source)
XLA Modules:
  0.0 654.4 jit_solution(14057767629468755891)
XLA Ops:
  9.2 55.6 %all-gather.3.cloned.1.call-done = bf16[512,4096]{1,0:T(8,128)(2,1)} async-done(((bf16[32,4096]{1,0:T(8,128)(2,1)}), bf16[512,4096]{1,0:T(8,128)(2,1)}) %all-gather.3.cloned.1.call-update) | async-done | bytes 4194320 | tf_op jit(solution)/shard_map/all_gather | solution.py:48
  67.5 46.2 %while.41 = (s32[]{:T(128)}, f32[512,448]{0,1:T(8,128)S(1)}, f32[512,448]{0,1:T(8,128)S(1)}, bf16[512,448]{0,1:T(8,128)(2,1)S(1)}, bf16[512,4096]{1,0:T(8,128)(2...) while((s32[]{:T(128)}, f32[512,448]{0,1:T(8,128)S(1)}, ...), condition=%wide.region_4.5_spmd, body=%wide.region_3.4_spmd.sunk | while | flops 1409687552 | bytes 46288932 | solution.py:73
  70.1 3.6 constant_dynamic-update-slice_fusion.7
  73.7 3.5 constant_dynamic-update-slice_fusion.6
  81.6 3.6 constant_dynamic-update-slice_fusion.7
  85.2 3.5 constant_dynamic-update-slice_fusion.6
  93.2 3.6 constant_dynamic-update-slice_fusion.7
  96.8 3.5 constant_dynamic-update-slice_fusion.6
  104.8 3.6 constant_dynamic-update-slice_fusion.7
  108.4 3.5 constant_dynamic-update-slice_fusion.6
  113.8 75.7 %reduce-scatter.6.cloned.1.call-done = bf16[32,4096]{1,0:T(8,128)(2,1)} async-done(((bf16[512,4096]{1,0:T(8,128)(2,1)}), bf16[32,4096]{1,0:T(8,128)(2,1)}) %reduce-scatter.6.cloned.1.call-update) | async-done | bytes 262160 | tf_op jit(solution)/shard_map/reduce_scatter | solution.py:76
  189.5 2.6 fusion.40
  192.3 52.6 %all-gather.5.cloned.1.call-done = bf16[512,4096]{1,0:T(8,128)(2,1)} async-done(((bf16[32,4096]{1,0:T(8,128)(2,1)}), bf16[512,4096]{1,0:T(8,128)(2,1)}) %all-gather.5.cloned.1.call-update) | async-done | bytes 4194320 | tf_op jit(solution)/shard_map/all_gather | solution.py:82
  247.3 7.0 %broadcast.181.clone = f32[2,4096,448]{1,2,0:T(8,128)} broadcast(f32[]{:T(128)} %constant.252.clone.1), dimensions={} | broadcast | bytes 14680068 | tf_op jit(solution)/shard_map/broadcast.15
  254.4 7.0 %broadcast.181 = f32[2,4096,448]{1,2,0:T(8,128)} broadcast(f32[]{:T(128)} %constant.252.clone.1), dimensions={} | broadcast | bytes 14680068 | tf_op jit(solution)/shard_map/broadcast.15
  261.4 7.0 %broadcast_in_dim.91 = f32[2,448,4096]{2,1,0:T(8,128)} broadcast(f32[]{:T(128)} %constant.252.clone.1), dimensions={} | broadcast | bytes 14680068 | tf_op jit(solution)/shard_map/broadcast_in_dim | solution.py:127
  268.5 152.3 %while.42 = (s32[]{:T(128)}, bf16[512,4096]{1,0:T(8,128)(2,1)}, f32[2,4096,448]{1,2,0:T(8,128)}, f32[2,4096,448]{1,2,0:T(8,128)}, f32[2,448,4096]{2,1,0:T(8,128)...) while((s32[]{:T(128)}, bf16[512,4096]{1,0:T(8,128)(2,1)}, ...), condition=%wide.region_9.10_spmd, body=%wide.region_7.9_spmd.sunk | while | flops 2830966784 | bytes 318461312 | solution.py:129
  271.7 3.6 select_convert_fusion.5
  275.4 3.6 fusion.81
  278.9 4.5 fusion.82
  285.9 2.7 copy-done.2
  291.0 2.8 copy-done.1
  293.8 12.7 %fusion.85 = f32[2,448,4096]{2,1,0:T(8,128)} fusion(f32[2,448,4096]{2,1,0:T(8,128)} %get-tuple-element.859, s32[]{:T(128)} %select_n.120, pred[]{:T(512)} %and_reduce_fusion.3, bf16[512,4096]{1,0:T(8,128)(2,1)} %get-tuple-element.883, s32[]{:T(128)S(6)} %select_n.119, bf16[512,448]{0,1:T(8,128)(2,1)S(1)} %get-tuple-element.891), kind=kOutput, calls=%fused_computation.25.clone.1 | convolution fusion | flops 473432064 | bytes 15845376 | tf_op jit(solution)/shard_map/while/body/eval_jaxpr/dot_general | solution.py:25
  309.8 3.6 select_convert_fusion.5
  313.4 3.6 fusion.81
  317.0 4.5 fusion.82
  324.0 2.7 copy-done.2
  329.0 2.8 copy-done.1
  331.9 12.8 %fusion.85 = f32[2,448,4096]{2,1,0:T(8,128)} fusion(f32[2,448,4096]{2,1,0:T(8,128)} %get-tuple-element.859, s32[]{:T(128)} %select_n.120, pred[]{:T(512)} %and_reduce_fusion.3, bf16[512,4096]{1,0:T(8,128)(2,1)} %get-tuple-element.883, s32[]{:T(128)S(6)} %select_n.119, bf16[512,448]{0,1:T(8,128)(2,1)S(1)} %get-tuple-element.891), kind=kOutput, calls=%fused_computation.25.clone.1 | convolution fusion | flops 473432064 | bytes 15845376 | tf_op jit(solution)/shard_map/while/body/eval_jaxpr/dot_general | solution.py:25
  347.9 3.6 select_convert_fusion.5
  351.6 3.6 fusion.81
  355.1 4.5 fusion.82
  362.1 2.7 copy-done.2
  367.1 2.8 copy-done.1
  370.0 12.8 %fusion.85 = f32[2,448,4096]{2,1,0:T(8,128)} fusion(f32[2,448,4096]{2,1,0:T(8,128)} %get-tuple-element.859, s32[]{:T(128)} %select_n.120, pred[]{:T(512)} %and_reduce_fusion.3, bf16[512,4096]{1,0:T(8,128)(2,1)} %get-tuple-element.883, s32[]{:T(128)S(6)} %select_n.119, bf16[512,448]{0,1:T(8,128)(2,1)S(1)} %get-tuple-element.891), kind=kOutput, calls=%fused_computation.25.clone.1 | convolution fusion | flops 473432064 | bytes 15845376 | tf_op jit(solution)/shard_map/while/body/eval_jaxpr/dot_general | solution.py:25
  386.0 3.6 select_convert_fusion.5
  389.6 3.6 fusion.81
  393.2 4.4 fusion.82
  400.1 2.7 copy-done.2
  405.2 2.8 copy-done.1
  408.0 12.8 %fusion.85 = f32[2,448,4096]{2,1,0:T(8,128)} fusion(f32[2,448,4096]{2,1,0:T(8,128)} %get-tuple-element.859, s32[]{:T(128)} %select_n.120, pred[]{:T(512)} %and_reduce_fusion.3, bf16[512,4096]{1,0:T(8,128)(2,1)} %get-tuple-element.883, s32[]{:T(128)S(6)} %select_n.119, bf16[512,448]{0,1:T(8,128)(2,1)S(1)} %get-tuple-element.891), kind=kOutput, calls=%fused_computation.25.clone.1 | convolution fusion | flops 473432064 | bytes 15845376 | tf_op jit(solution)/shard_map/while/body/eval_jaxpr/dot_general | solution.py:25
  420.9 9.3 %convert_element_type.63 = bf16[2,448,4096]{2,1,0:T(8,128)(2,1)} convert(f32[2,448,4096]{2,1,0:T(8,128)} %get-tuple-element.513) | non-fusion elementwise | flops 3670016 | bytes 22020096 | tf_op jit(solution)/shard_map/convert_element_type | solution.py:142
  430.2 9.3 %convert_element_type.61 = bf16[2,4096,448]{1,2,0:T(8,128)(2,1)} convert(f32[2,4096,448]{1,2,0:T(8,128)} %get-tuple-element.511) | non-fusion elementwise | flops 3670016 | bytes 22020096 | tf_op jit(solution)/shard_map/convert_element_type | solution.py:136
  439.6 9.7 %convert_element_type.62 = bf16[2,4096,448]{1,2,0:T(8,128)(2,1)} convert(f32[2,4096,448]{1,2,0:T(8,128)} %get-tuple-element.512) | non-fusion elementwise | flops 3670016 | bytes 22020096 | tf_op jit(solution)/shard_map/convert_element_type | solution.py:139
  449.3 47.3 %reduce-scatter.8.cloned.1.call-done = bf16[32,4096]{1,0:T(8,128)(2,1)} async-done(((bf16[512,4096]{1,0:T(8,128)(2,1)}), bf16[32,4096]{1,0:T(8,128)(2,1)}) %reduce-scatter.8.cloned.1.call-update) | async-done | bytes 262160 | tf_op jit(solution)/shard_map/reduce_scatter | solution.py:131
  496.6 50.8 %reduce-scatter.14.cloned.1.call-done = bf16[2,448,512]{2,1,0:T(8,128)(2,1)} async-done(((bf16[2,448,4096]{2,1,0:T(8,128)(2,1)}), bf16[2,448,512]{2,1,0:T(8,128)(2,1)}) %reduce-scatter.14.cloned.1.call-update) | async-done | bytes 917520 | tf_op jit(solution)/shard_map/reduce_scatter | solution.py:141
  547.4 50.0 %reduce-scatter.10.cloned.1.call-done = bf16[2,512,448]{1,2,0:T(8,128)(2,1)} async-done(((bf16[2,4096,448]{1,2,0:T(8,128)(2,1)}), bf16[2,512,448]{1,2,0:T(8,128)(2,1)}) %reduce-scatter.10.cloned.1.call-update) | async-done | bytes 917520 | tf_op jit(solution)/shard_map/reduce_scatter | solution.py:135
  597.4 50.1 %reduce-scatter.12.cloned.1.call-done = bf16[2,512,448]{1,2,0:T(8,128)(2,1)} async-done(((bf16[2,4096,448]{1,2,0:T(8,128)(2,1)}), bf16[2,512,448]{1,2,0:T(8,128)(2,1)}) %reduce-scatter.12.cloned.1.call-update) | async-done | bytes 917520 | tf_op jit(solution)/shard_map/reduce_scatter | solution.py:138
  (108 shorter events, 42.0 us)
Async XLA Ops:
  7.2 57.6 %all-gather.3.cloned.1.call-start = ((), (), s32[]{:S(2)}) async-start(), calls=%async_computation.5 | async-start | bytes 4456448 | tf_op jit(solution)/shard_map/all_gather | solution.py:48
  7.9 181.6 %reduce-scatter.6.cloned.1.call-start = ((), (), s32[]{:S(2)}) async-start(), calls=%async_computation.6 | async-start | bytes 4456448 | tf_op jit(solution)/shard_map/reduce_scatter | solution.py:76
  67.5 122.0 %copy-start.6 = (bf16[32,4096]{1,0:T(8,128)(2,1)S(1)}, bf16[32,4096]{1,0:T(8,128)(2,1)}, u32[]{:S(2)}) copy-start(bf16[32,4096]{1,0:T(8,128)(2,1)} %param.18) | copy-start | bytes 786436
  67.5 122.0 %copy-start.8 = (f32[32]{0:T(128)S(1)}, f32[32]{0:T(128)}, u32[]{:S(2)}) copy-start(f32[32]{0:T(128)} %param.19) | copy-start | bytes 388
  70.0 7.3 %copy-start.5 = (bf16[2,448,4096]{2,1,0:T(8,128)(2,1)S(1)}, bf16[2,448,4096]{2,1,0:T(8,128)(2,1)}, u32[]{:S(2)}) copy-start(bf16[2,448,4096]{2,1,0:T(8,128)(2,1)} %get-tuple-element.827) | copy-start | bytes 22020100 | tf_op jit(solution)/shard_map/while
  81.6 7.3 %copy-start.5 = (bf16[2,448,4096]{2,1,0:T(8,128)(2,1)S(1)}, bf16[2,448,4096]{2,1,0:T(8,128)(2,1)}, u32[]{:S(2)}) copy-start(bf16[2,448,4096]{2,1,0:T(8,128)(2,1)} %get-tuple-element.827) | copy-start | bytes 22020100 | tf_op jit(solution)/shard_map/while
  93.2 7.3 %copy-start.5 = (bf16[2,448,4096]{2,1,0:T(8,128)(2,1)S(1)}, bf16[2,448,4096]{2,1,0:T(8,128)(2,1)}, u32[]{:S(2)}) copy-start(bf16[2,448,4096]{2,1,0:T(8,128)(2,1)} %get-tuple-element.827) | copy-start | bytes 22020100 | tf_op jit(solution)/shard_map/while
  104.7 7.3 %copy-start.5 = (bf16[2,448,4096]{2,1,0:T(8,128)(2,1)S(1)}, bf16[2,448,4096]{2,1,0:T(8,128)(2,1)}, u32[]{:S(2)}) copy-start(bf16[2,448,4096]{2,1,0:T(8,128)(2,1)} %get-tuple-element.827) | copy-start | bytes 22020100 | tf_op jit(solution)/shard_map/while
  113.8 131.1 %all-gather.5.cloned.1.call-start = ((), (), s32[]{:S(2)}) async-start(), calls=%async_computation.7 | async-start | bytes 4456448 | tf_op jit(solution)/shard_map/all_gather | solution.py:82
  192.1 304.5 %reduce-scatter.8.cloned.1.call-start = ((), (), s32[]{:S(2)}) async-start(), calls=%async_computation.8 | async-start | bytes 4456448 | tf_op jit(solution)/shard_map/reduce_scatter | solution.py:131
  261.4 7.1 %copy-start.7 = (s32[3]{0:T(128)S(1)}, s32[3]{0:T(128)}, u32[]{:S(2)}) copy-start(s32[3]{0:T(128)} %constant.248.clone.1) | copy-start | bytes 40
  271.7 11.7 %copy-start = (f32[2,4096,448]{1,2,0:T(8,128)S(1)}, f32[2,4096,448]{1,2,0:T(8,128)}, u32[]{:S(2)}) copy-start(f32[2,4096,448]{1,2,0:T(8,128)} %get-tuple-element.858) | copy-start | bytes 44040196 | tf_op jit(solution)/shard_map/while
  275.3 8.1 %copy-start.4 = (bf16[512,4096]{1,0:T(8,128)(2,1)S(1)}, bf16[512,4096]{1,0:T(8,128)(2,1)}, u32[]{:S(2)}) copy-start(bf16[512,4096]{1,0:T(8,128)(2,1)} %get-tuple-element.890) | copy-start | bytes 12582916 | tf_op jit(solution)/shard_map/while
  283.4 5.2 copy-start.2
  288.6 5.2 copy-start.1
  293.8 12.7 %copy-start.3 = (f32[2,4096,448]{1,2,0:T(8,128)}, f32[2,4096,448]{1,2,0:T(8,128)S(1)}, u32[]{:S(2)}) copy-start(f32[2,4096,448]{1,2,0:T(8,128)S(1)} %fusion.83) | copy-start | bytes 44040196 | tf_op jit(solution)/shard_map/while
  309.8 11.7 %copy-start = (f32[2,4096,448]{1,2,0:T(8,128)S(1)}, f32[2,4096,448]{1,2,0:T(8,128)}, u32[]{:S(2)}) copy-start(f32[2,4096,448]{1,2,0:T(8,128)} %get-tuple-element.858) | copy-start | bytes 44040196 | tf_op jit(solution)/shard_map/while
  313.4 8.1 %copy-start.4 = (bf16[512,4096]{1,0:T(8,128)(2,1)S(1)}, bf16[512,4096]{1,0:T(8,128)(2,1)}, u32[]{:S(2)}) copy-start(bf16[512,4096]{1,0:T(8,128)(2,1)} %get-tuple-element.890) | copy-start | bytes 12582916 | tf_op jit(solution)/shard_map/while
  321.5 5.2 copy-start.2
  326.7 5.2 copy-start.1
  331.9 12.8 %copy-start.3 = (f32[2,4096,448]{1,2,0:T(8,128)}, f32[2,4096,448]{1,2,0:T(8,128)S(1)}, u32[]{:S(2)}) copy-start(f32[2,4096,448]{1,2,0:T(8,128)S(1)} %fusion.83) | copy-start | bytes 44040196 | tf_op jit(solution)/shard_map/while
  347.9 11.7 %copy-start = (f32[2,4096,448]{1,2,0:T(8,128)S(1)}, f32[2,4096,448]{1,2,0:T(8,128)}, u32[]{:S(2)}) copy-start(f32[2,4096,448]{1,2,0:T(8,128)} %get-tuple-element.858) | copy-start | bytes 44040196 | tf_op jit(solution)/shard_map/while
  351.5 8.0 %copy-start.4 = (bf16[512,4096]{1,0:T(8,128)(2,1)S(1)}, bf16[512,4096]{1,0:T(8,128)(2,1)}, u32[]{:S(2)}) copy-start(bf16[512,4096]{1,0:T(8,128)(2,1)} %get-tuple-element.890) | copy-start | bytes 12582916 | tf_op jit(solution)/shard_map/while
  359.6 5.2 copy-start.2
  364.8 5.2 copy-start.1
  370.0 12.8 %copy-start.3 = (f32[2,4096,448]{1,2,0:T(8,128)}, f32[2,4096,448]{1,2,0:T(8,128)S(1)}, u32[]{:S(2)}) copy-start(f32[2,4096,448]{1,2,0:T(8,128)S(1)} %fusion.83) | copy-start | bytes 44040196 | tf_op jit(solution)/shard_map/while
  386.0 11.7 %copy-start = (f32[2,4096,448]{1,2,0:T(8,128)S(1)}, f32[2,4096,448]{1,2,0:T(8,128)}, u32[]{:S(2)}) copy-start(f32[2,4096,448]{1,2,0:T(8,128)} %get-tuple-element.858) | copy-start | bytes 44040196 | tf_op jit(solution)/shard_map/while
  389.6 8.0 %copy-start.4 = (bf16[512,4096]{1,0:T(8,128)(2,1)S(1)}, bf16[512,4096]{1,0:T(8,128)(2,1)}, u32[]{:S(2)}) copy-start(bf16[512,4096]{1,0:T(8,128)(2,1)} %get-tuple-element.890) | copy-start | bytes 12582916 | tf_op jit(solution)/shard_map/while
  397.6 5.2 copy-start.2
  402.8 5.2 copy-start.1
  408.0 12.8 %copy-start.3 = (f32[2,4096,448]{1,2,0:T(8,128)}, f32[2,4096,448]{1,2,0:T(8,128)S(1)}, u32[]{:S(2)}) copy-start(f32[2,4096,448]{1,2,0:T(8,128)S(1)} %fusion.83) | copy-start | bytes 44040196 | tf_op jit(solution)/shard_map/while
  420.8 126.6 %reduce-scatter.14.cloned.1.call-start = ((), (), s32[]{:S(2)}) async-start(), calls=%async_computation.11 | async-start | bytes 8257536 | tf_op jit(solution)/shard_map/reduce_scatter | solution.py:141
  430.2 167.3 %reduce-scatter.10.cloned.1.call-start = ((), (), s32[]{:S(2)}) async-start(), calls=%async_computation.9 | async-start | bytes 8257536 | tf_op jit(solution)/shard_map/reduce_scatter | solution.py:135
  439.6 208.0 %reduce-scatter.12.cloned.1.call-start = ((), (), s32[]{:S(2)}) async-start(), calls=%async_computation.10 | async-start | bytes 8257536 | tf_op jit(solution)/shard_map/reduce_scatter | solution.py:138
Sparse Core Ops, SparseCore 0:
  10.1 54.5 all-gather.2
  113.9 75.5 reduce-scatter.5
  192.4 52.4 all-gather.4
  420.9 75.6 reduce-scatter.7
  499.4 47.9 reduce-scatter.13
  550.3 47.1 reduce-scatter.9
  600.4 47.1 reduce-scatter.11
where the time goes:
time: 655 us; the launch traced here: 654 us
  waiting for transfers between devices  383 us (58%)
  matrix products  152 us (23%)
  local copies, waits for them, and re-layouts  53.3 us (8%)
  other arithmetic  35.4 us (5%)
  loops' own time  15.9 us (2%)
  between operations  14.2 us (2%)
    reduce_scatter x1, waiting for transfers between devices, per_device(): lax.psum_scatter(share_all.astype(jnp.bfloat16), 'et', scatter_dimension=...  75.7 us
    dot_general x12, matrix products, contract_rows(): lax.dot_general(left, right, (((0,), (0,)), ((), ())), preferred_element_...  70.3 us
    all_gather x1, waiting for transfers between devices, per_device(): gathered = lax.all_gather(routed_rows, 'et', axis=0, tiled=True)  55.6 us
    all_gather x1, waiting for transfers between devices, per_device(): scaled = lax.all_gather(scaled_local, 'et', axis=0, tiled=True)  52.6 us
    reduce_scatter x1, waiting for transfers between devices, per_device(): lax.psum_scatter(backward[5].astype(jnp.bfloat16), 'dp', scatter_dimensio...  50.8 us
    reduce_scatter x1, waiting for transfers between devices, per_device(): lax.psum_scatter(backward[4].astype(jnp.bfloat16), 'dp', scatter_dimensio...  50.1 us
    reduce_scatter x1, waiting for transfers between devices, per_device(): lax.psum_scatter(backward[3].astype(jnp.bfloat16), 'dp', scatter_dimensio...  50 us
    reduce_scatter x1, waiting for transfers between devices, per_device(): lax.psum_scatter(rows_all.astype(jnp.bfloat16), 'et', scatter_dimension=0...  47.3 us
  transfers between devices with their start and end apart: 7, of which 7 were waited for; matrix products, arithmetic and copies ran while one was open for 5% of the time, Pallas kernels for 0%

commit v1 on v0

v1 whole, which is shorter than its diff:
```python
import functools

import jax
import jax.numpy as jnp
from jax import lax
from jax.experimental import pallas as pl
from jax.experimental.pallas import tpu as pltpu
from jax.sharding import PartitionSpec as P

MESH = pl.DeviceIdType.MESH
BF = jnp.bfloat16
F32 = jnp.float32
GROUPS, SLOTS, OWN, DM, HID = 8, 512, 32, 4096, 448
DS = DM // GROUPS
ROWS = GROUPS * SLOTS
BR = 256
RMAX = ROWS + BR
LEVELS = (1536, 1792, 2048, RMAX)
VLIM = 60 * 1024 * 1024


def rcopy(src, dst, ssem, rsem, dev):
    return pltpu.make_async_remote_copy(
        src_ref=src, dst_ref=dst, send_sem=ssem, recv_sem=rsem,
        device_id=dev, device_id_type=MESH,
    )


def greet(peers):
    bar = pltpu.get_barrier_semaphore()
    for dev in peers:
        pl.semaphore_signal(bar, inc=1, device_id=dev, device_id_type=MESH)
    pl.semaphore_wait(bar, len(peers))


def plane(axis, pos, j):
    y, x = j // 4, j % 4
    return {"et": y * 4 + pos % 4} if axis == "x" else {"et": (pos % 4) * 4 + x}


def gather_kernel(rows_ref, sc_ref, xg, sg, psend, precv, osem, rsend, rrecv):
    d, j = lax.axis_index("dp"), lax.axis_index("et")
    y, x = j // 4, j % 4
    greet([{"dp": (d + k) % 8} for k in range(1, 8)]
          + [plane("x", x + 1, j), plane("x", x + 3, j), plane("y", y + 1, j), plane("y", y + 3, j)])
    arrays = []
    for a, (src, out, first, second) in enumerate(
        ((rows_ref, xg, "x", "y"), (sc_ref, sg, "y", "x"))
    ):
        p, q = (x, y) if first == "x" else (y, x)

        def blk(pp, qq, half=None, out=out, first=first):
            yy, xx = (qq % 4, pp % 4) if first == "x" else (pp % 4, qq % 4)
            g = slice(None) if half is None else pl.ds(4 * half, 4)
            return out.at[g, yy, xx]

        def send(i, ref, axis, pos, a=a):
            c = rcopy(ref, ref, rsend.at[a, i], rrecv.at[a, i], plane(axis, pos, j))
            c.start()
            return c

        cps = []
        for k in range(1, 8):
            dd = (d + k) % 8
            c = rcopy(src.at[:, pl.ds(dd * DS, DS)], out.at[d, y, x],
                      psend.at[a, k - 1], precv.at[a, k - 1], {"dp": dd})
            c.start()
            cps.append(c)
        own = pltpu.make_async_copy(src.at[:, pl.ds(d * DS, DS)], out.at[d, y, x], osem.at[a])
        own.start()
        arrays.append((p, q, first, second, blk, send, cps, own))

    sent = [dict(), dict()]

    def second_sends(a, u):
        p, q, first, second, blk, send, cps, own = arrays[a]
        base = 4 + 4 * (u % 4)
        sent[a][base] = send(base, blk(p + u, q), second, q + 1)
        sent[a][base + 1] = send(base + 1, blk(p + u, q), second, q + 3)

    def second_forward(a, u):
        p, q, first, second, blk, send, cps, own = arrays[a]
        base = 4 + 4 * (u % 4)
        sent[a][base].wait_recv()
        sent[a][base + 2] = send(base + 2, blk(p + u, q + 3, 0), second, q + 1)
        sent[a][base + 1].wait_recv()
        sent[a][base + 3] = send(base + 3, blk(p + u, q + 1, 1), second, q + 3)

    for a in range(2):
        p, q, first, second, blk, send, cps, own = arrays[a]
        own.wait()
        for c in cps:
            c.wait_recv()
        sent[a][0] = send(0, blk(p, q), first, p + 1)
        sent[a][1] = send(1, blk(p, q), first, p + 3)
        second_sends(a, 0)
    for a in range(2):
        p, q, first, second, blk, send, cps, own = arrays[a]
        sent[a][0].wait_recv()
        sent[a][2] = send(2, blk(p + 3, q, 0), first, p + 1)
        second_sends(a, 3)
        sent[a][1].wait_recv()
        sent[a][3] = send(3, blk(p + 1, q, 1), first, p + 3)
        second_sends(a, 1)
    for a in range(2):
        second_forward(a, 0)
    for a in range(2):
        sent[a][2].wait_recv()
        sent[a][3].wait_recv()
        second_sends(a, 2)
    for u in (3, 1, 2):
        for a in range(2):
            second_forward(a, u)
    for a in range(2):
        for u in range(4):
            sent[a][6 + 4 * u].wait_recv()
            sent[a][7 + 4 * u].wait_recv()
        for c in arrays[a][6]:
            c.wait_send()
        for c in sent[a].values():
            c.wait_send()


def gather_rows(rows, scaled):
    shape = jax.ShapeDtypeStruct((GROUPS, 4, 4, OWN, DS), BF)
    return pl.pallas_call(
        gather_kernel,
        out_shape=(shape, shape),
        in_specs=[pl.BlockSpec(memory_space=pltpu.VMEM)] * 2,
        out_specs=(pl.BlockSpec(memory_space=pl.ANY),) * 2,
        scratch_shapes=[
            pltpu.SemaphoreType.DMA((2, 7)),
            pltpu.SemaphoreType.DMA((2, 7)),
            pltpu.SemaphoreType.DMA((2,)),
            pltpu.SemaphoreType.DMA((2, 20)),
            pltpu.SemaphoreType.DMA((2, 20)),
        ],
        compiler_params=pltpu.CompilerParams(
            collective_id=0, has_side_effects=True, vmem_limit_bytes=VLIM),
        name="gather_rows",
    )(rows, scaled)


def segments(cnt):
    segs, t = [], 0
    ends = []
    for e in range(2):
        row = []
        for g in range(GROUPS):
            c = cnt[g, e]
            first = 0 if e == 0 else (cnt[g, 0] + 127) // 128 * 128
            n = (c + 15) // 16
            row.append((c, first, n, t))
            t = t + n
        ends.append(t)
        t = (t + BR // 16 - 1) // (BR // 16) * (BR // 16)
        ends.append(t)
        segs.append(row)
    return segs, ends


def tile(i):
    return pl.ds(pl.multiple_of(i * 16, 16), 16)


def first_kernel(cnt, xg, sg, wg, wu, wd, part, xc_o, sc_o,
                 xv, sv, xc, sc, wgv, wuv, wdv, pv, rsem, wsem, osem):
    d = lax.axis_index("dp")
    cols = pl.ds(pl.multiple_of(d * DS, DS), DS)
    segs, ends = segments(cnt)
    wcp = [pltpu.make_async_copy(wg.at[:, cols, :], wgv, wsem.at[0]),
           pltpu.make_async_copy(wu.at[:, cols, :], wuv, wsem.at[1]),
           pltpu.make_async_copy(wd.at[:, :, cols], wdv, wsem.at[2])]

    def block_copies(g, b):
        rows = pl.ds(g * SLOTS + b * 128, 128)
        return (pltpu.make_async_copy(xg.at[rows], xv.at[rows], rsem.at[0, g * 4 + b]),
                pltpu.make_async_copy(sg.at[rows], sv.at[rows], rsem.at[1, g * 4 + b]))

    for start in (True, False):
        for g in range(GROUPS):
            used = (cnt[g, 0] + 127) // 128 + (cnt[g, 1] + 127) // 128
            for b in range(4):
                @pl.when(b < used)
                def _(g=g, b=b, start=start):
                    for c in block_copies(g, b):
                        if start:
                            c.start()
                        else:
                            c.wait()
        if start:
            for c in wcp:
                c.start()

    zeros = jnp.zeros((16, DS), BF)
    iota = lax.broadcasted_iota(jnp.int32, (16, DS), 0)
    for e in range(2):
        for g in range(GROUPS):
            c, first, n, t0 = segs[e][g]
            s0 = g * (SLOTS // 16) + first // 16

            def move(k, _, s0=s0, t0=t0):
                xc[tile(t0 + k), :] = xv[tile(s0 + k), :]
                sc[tile(t0 + k), :] = sv[tile(s0 + k), :]
                return 0

            lax.fori_loop(0, n - 1, move, 0)
            keep = iota < c - 16 * (n - 1)
            xt = xv[tile(s0 + n - 1), :].astype(F32)
            st = sv[tile(s0 + n - 1), :].astype(F32)
            xc[tile(t0 + n - 1), :] = jnp.where(keep, xt, 0.0).astype(BF)
            sc[tile(t0 + n - 1), :] = jnp.where(keep, st, 0.0).astype(BF)

        def blank(t, _):
            xc[tile(t), :] = zeros
            sc[tile(t), :] = zeros
            return 0

        lax.fori_loop(ends[2 * e], ends[2 * e + 1], blank, 0)
    for c in wcp:
        c.wait()
    nb0, nb = ends[1] // (BR // 16), ends[3] // (BR // 16)

    def out_copies(b):
        rows = pl.ds(pl.multiple_of(b * BR, BR), BR)
        return (pltpu.make_async_copy(pv.at[:, rows], part.at[:, rows], osem.at[0]),
                pltpu.make_async_copy(xc.at[rows], xc_o.at[rows], osem.at[1]),
                pltpu.make_async_copy(sc.at[rows], sc_o.at[rows], osem.at[2]))

    def block(b, _):
        e = (b >= nb0).astype(jnp.int32)
        rows = pl.ds(pl.multiple_of(b * BR, BR), BR)
        xb, sb = xc[rows, :], sc[rows, :]
        pv[0, rows, :] = jnp.dot(xb, wgv[e], preferred_element_type=F32).astype(BF)
        pv[1, rows, :] = jnp.dot(xb, wuv[e], preferred_element_type=F32).astype(BF)
        pv[2, rows, :] = lax.dot_general(
            sb, wdv[e], (((1,), (1,)), ((), ())), preferred_element_type=F32).astype(BF)
        for c in out_copies(b):
            c.start()
        return 0

    lax.fori_loop(0, nb, block, 0)

    def drain(b, _):
        for c in out_copies(b):
            c.wait()
        return 0

    lax.fori_loop(0, nb, drain, 0)


def first_matmuls(counts, xg, sg, wg, wu, wd):
    any_ = pl.BlockSpec(memory_space=pl.ANY)
    return pl.pallas_call(
        first_kernel,
        out_shape=(jax.ShapeDtypeStruct((3, RMAX, HID), BF),
                   jax.ShapeDtypeStruct((RMAX, DS), BF),
                   jax.ShapeDtypeStruct((RMAX, DS), BF)),
        in_specs=[pl.BlockSpec(memory_space=pltpu.SMEM)] + [any_] * 5,
        out_specs=(any_,) * 3,
        scratch_shapes=[
            pltpu.VMEM((ROWS, DS), BF), pltpu.VMEM((ROWS, DS), BF),
            pltpu.VMEM((RMAX, DS), BF), pltpu.VMEM((RMAX, DS), BF),
            pltpu.VMEM((2, DS, HID), BF), pltpu.VMEM((2, DS, HID), BF), pltpu.VMEM((2, HID, DS), BF),
            pltpu.VMEM((3, RMAX, HID), BF),
            pltpu.SemaphoreType.DMA((2, 32)), pltpu.SemaphoreType.DMA((3,)),
            pltpu.SemaphoreType.DMA((3,)),
        ],
        compiler_params=pltpu.CompilerParams(vmem_limit_bytes=VLIM),
        name="first_matmuls",
    )(counts, xg, sg, wg, wu, wd)


def exchange_kernel(r, p, h, own, prt, q, l1, r1, s1, s2, l2, r2, res,
                    osem, psend, precv, bsend, brecv, gsend, grecv, lsem):
    d = lax.axis_index("dp")
    z, c = d // 2, d % 2
    r8, r16 = r // 8, r // 16
    up, down = {"dp": (z + 1) % 4 * 2 + c}, {"dp": (z + 3) % 4 * 2 + c}
    mate = {"dp": z * 2 + 1 - c}
    greet([up, down, mate])

    def rows(zz, cc):
        return pl.ds(pl.multiple_of((zz % 4 * 2 + cc) * r8, r16), r8)

    def half(zz, cc, i):
        return pl.ds(pl.multiple_of((zz % 4 * 2 + cc) * r8 + i * r16, r16), r16)

    first, second = pl.ds(0, r16), pl.ds(r16, r16)
    order = (2, 1, 3, 0)
    pair, mine = {}, {}
    for i in order:
        pair[i] = rcopy(p.at[:, rows(z + i, 1 - c)], prt.at[i], psend.at[i], precv.at[i], mate)
        pair[i].start()
        mine[i] = pltpu.make_async_copy(p.at[:, rows(z + i, c)], own.at[i], osem.at[i])
        mine[i].start()

    def bsum(i):
        mine[i].wait()
        pair[i].wait_recv()
        for k in range(3):
            q[i, k] = (own[i, k].astype(F32) + prt[i, k].astype(F32)).astype(BF)

    cps = []

    def push(i, src, dst, dev):
        cp = rcopy(src, dst, bsend.at[i], brecv.at[i], dev)
        cp.start()
        cps.append(cp)
        return cp

    bsum(2)
    a_l = push(0, q.at[2, :, first], l1, up)
    a_r = push(1, q.at[2, :, second], r1, down)
    bsum(1)
    b_l2 = push(2, q.at[1, :, second], l2.at[:, second], up)
    bsum(3)
    b_r1 = push(3, q.at[3, :, first], r2.at[:, first], down)
    a_l.wait_recv()
    for k in range(3):
        s1[k] = (l1[k].astype(F32) + q[1, k, 0:r16].astype(F32)).astype(BF)
    b_l1 = push(4, s1, l2.at[:, first], up)
    a_r.wait_recv()
    for k in range(3):
        s2[k] = (r1[k].astype(F32) + q[3, k, r16:r8].astype(F32)).astype(BF)
    b_r2 = push(5, s2, r2.at[:, second], down)
    mine[0].wait()
    pair[0].wait_recv()
    for cp in (b_l2, b_r1, b_l1, b_r2):
        cp.wait_recv()

    def total(k):
        return (own[0, k].astype(F32) + prt[0, k].astype(F32)
                + l2[k].astype(F32) + r2[k].astype(F32))

    gate, lin, grad = total(0), total(1), total(2)
    s = 1.0 / (1.0 + jnp.exp(-gate))
    act = gate * s
    res[0] = (act * lin).astype(BF)
    res[1] = (grad * lin * s * (1.0 + gate * (1.0 - s))).astype(BF)
    res[2] = (grad * act).astype(BF)

    keep = pltpu.make_async_copy(res, h.at[:, rows(z, c)], lsem)
    keep.start()
    gps = {}

    def spread(i, src, dst, dev):
        cp = rcopy(src, dst, gsend.at[i], grecv.at[i], dev)
        cp.start()
        gps[i] = cp

    spread(0, res, h.at[:, rows(z, c)], up)
    spread(1, res, h.at[:, rows(z, c)], down)
    spread(2, res, h.at[:, rows(z, c)], mate)
    gps[0].wait_recv()
    spread(3, h.at[:, half(z + 3, c, 0)], h.at[:, half(z + 3, c, 0)], up)
    spread(4, h.at[:, rows(z + 3, c)], h.at[:, rows(z + 3, c)], mate)
    gps[1].wait_recv()
    spread(5, h.at[:, half(z + 1, c, 1)], h.at[:, half(z + 1, c, 1)], down)
    spread(6, h.at[:, rows(z + 1, c)], h.at[:, rows(z + 1, c)], mate)
    gps[3].wait_recv()
    spread(7, h.at[:, half(z + 2, c, 0)], h.at[:, half(z + 2, c, 0)], mate)
    gps[5].wait_recv()
    spread(8, h.at[:, half(z + 2, c, 1)], h.at[:, half(z + 2, c, 1)], mate)
    for i in (2, 4, 6, 7, 8):
        gps[i].wait_recv()
    keep.wait()
    for cp in list(pair.values()) + cps + list(gps.values()):
        cp.wait_send()


def exchange(r, cid, part):
    r8, r16 = r // 8, r // 16
    any_ = pl.BlockSpec(memory_space=pl.ANY)
    v = lambda *s: pltpu.VMEM(s, BF)
    dma = lambda n: pltpu.SemaphoreType.DMA((n,))
    return pl.pallas_call(
        functools.partial(exchange_kernel, r),
        out_shape=jax.ShapeDtypeStruct((3, RMAX, HID), BF),
        in_specs=[any_],
        out_specs=any_,
        scratch_shapes=[
            v(4, 3, r8, HID), v(4, 3, r8, HID), v(4, 3, r8, HID),
            v(3, r16, HID), v(3, r16, HID), v(3, r16, HID), v(3, r16, HID),
            v(3, r8, HID), v(3, r8, HID), v(3, r8, HID),
            dma(4), dma(4), dma(4), dma(6), dma(6), dma(9), dma(9), pltpu.SemaphoreType.DMA,
        ],
        compiler_params=pltpu.CompilerParams(
            collective_id=cid, has_side_effects=True, vmem_limit_bytes=VLIM),
        name="exchange_%d" % r,
    )(part)


def second_kernel(cnt, h, xc_i, sc_i, wg, wu, wd, o, gr, dg, du, dd,
                  hv, xc, sc, wgv, wuv, wdv, ov, gv, ag, au, ad, bsem, wsem):
    d = lax.axis_index("dp")
    cols = pl.ds(pl.multiple_of(d * DS, DS), DS)
    segs, ends = segments(cnt)
    nb0, nb = ends[1] // (BR // 16), ends[3] // (BR // 16)
    wcp = [pltpu.make_async_copy(wg.at[:, cols, :], wgv, wsem.at[0]),
           pltpu.make_async_copy(wu.at[:, cols, :], wuv, wsem.at[1]),
           pltpu.make_async_copy(wd.at[:, :, cols], wdv, wsem.at[2])]

    def in_copies(b):
        rows = pl.ds(pl.multiple_of(b * BR, BR), BR)
        return (pltpu.make_async_copy(h.at[:, rows], hv.at[:, rows], bsem.at[0, b]),
                pltpu.make_async_copy(xc_i.at[rows], xc.at[rows], bsem.at[1, b]),
                pltpu.make_async_copy(sc_i.at[rows], sc.at[rows], bsem.at[2, b]))

    for c in wcp:
        c.start()

    def begin(b, _):
        for c in in_copies(b):
            c.start()
        return 0

    lax.fori_loop(0, nb, begin, 0)
    ag[...] = jnp.zeros_like(ag)
    au[...] = jnp.zeros_like(au)
    ad[...] = jnp.zeros_like(ad)
    for c in wcp:
        c.wait()
    tr = (((1,), (1,)), ((), ()))
    tl = (((0,), (0,)), ((), ()))

    def block(b, _):
        e = (b >= nb0).astype(jnp.int32)
        rows = pl.ds(pl.multiple_of(b * BR, BR), BR)
        for c in in_copies(b):
            c.wait()
        hb, gb, lb = hv[0, rows, :], hv[1, rows, :], hv[2, rows, :]
        ov[rows, :] = jnp.dot(hb, wdv[e], preferred_element_type=F32).astype(BF)
        gv[rows, :] = (lax.dot_general(gb, wgv[e], tr, preferred_element_type=F32)
                       + lax.dot_general(lb, wuv[e], tr, preferred_element_type=F32)).astype(BF)
        xb, sb = xc[rows, :], sc[rows, :]
        ag[e] += lax.dot_general(xb, gb, tl, preferred_element_type=F32)
        au[e] += lax.dot_general(xb, lb, tl, preferred_element_type=F32)
        ad[e] += lax.dot_general(hb, sb, tl, preferred_element_type=F32)
        return 0

    lax.fori_loop(0, nb, block, 0)
    dg[...] = ag[...].astype(BF)
    du[...] = au[...].astype(BF)
    dd[...] = ad[...].astype(BF)

    zeros = jnp.zeros((16, DS), BF)
    for g in range(GROUPS):
        base = g * (SLOTS // 16)
        stop = SLOTS // 16
        for e in (1, 0):
            c, first, n, t0 = segs[e][g]
            s0 = first // 16

            def move(k, _, base=base, s0=s0, t0=t0):
                o[tile(base + s0 + k), :] = ov[tile(t0 + k), :]
                gr[tile(base + s0 + k), :] = gv[tile(t0 + k), :]
                return 0

            def blank(k, _, base=base):
                o[tile(base + k), :] = zeros
                gr[tile(base + k), :] = zeros
                return 0

            lax.fori_loop(0, n, move, 0)
            lax.fori_loop(s0 + n, stop, blank, 0)
            stop = s0


def second_matmuls(counts, h, xc, sc, wg, wu, wd):
    any_ = pl.BlockSpec(memory_space=pl.ANY)
    vm = pl.BlockSpec(memory_space=pltpu.VMEM)
    s = jax.ShapeDtypeStruct
    return pl.pallas_call(
        second_kernel,
        out_shape=(s((ROWS, DS), BF), s((ROWS, DS), BF),
                   s((2, DS, HID), BF), s((2, DS, HID), BF), s((2, HID, DS), BF)),
        in_specs=[pl.BlockSpec(memory_space=pltpu.SMEM)] + [any_] * 6,
        out_specs=(vm,) * 5,
        scratch_shapes=[
            pltpu.VMEM((3, RMAX, HID), BF),
            pltpu.VMEM((RMAX, DS), BF), pltpu.VMEM((RMAX, DS), BF),
            pltpu.VMEM((2, DS, HID), BF), pltpu.VMEM((2, DS, HID), BF), pltpu.VMEM((2, HID, DS), BF),
            pltpu.VMEM((RMAX, DS), BF), pltpu.VMEM((RMAX, DS), BF),
            pltpu.VMEM((2, DS, HID), F32), pltpu.VMEM((2, DS, HID), F32), pltpu.VMEM((2, HID, DS), F32),
            pltpu.SemaphoreType.DMA((3, RMAX // BR)), pltpu.SemaphoreType.DMA((3,)),
        ],
        compiler_params=pltpu.CompilerParams(vmem_limit_bytes=VLIM),
        name="second_matmuls",
    )(counts, h, xc, sc, wg, wu, wd)


def reduce_kernel(o_ref, g_ref, rw_ref, oc_ref, out_o, out_w, out_g,
                  l1, r1, s1, s2, l2, r2, acc, bl1, br1, bs1, bs2, bl2, br2, fin, rec,
                  asend, arecv, bsend, brecv, psend, precv):
    d, j = lax.axis_index("dp"), lax.axis_index("et")
    y, x = j // 4, j % 4
    greet([{"dp": (d + k) % 8} for k in range(1, 8)]
          + [plane("x", x + 1, j), plane("x", x + 3, j), plane("y", y + 1, j), plane("y", y + 3, j)])
    lo, hi = pl.ds(0, 4), pl.ds(4, 4)
    order = (2, 1, 3, 0)
    info = []
    cps = []
    for a, (src, first) in enumerate(((o_ref, "y"), (g_ref, "x"))):
        second = "x" if first == "y" else "y"
        p, q = (y, x) if first == "y" else (x, y)

        def blk(pp, qq, g, src=src, first=first):
            yy, xx = (pp % 4, qq % 4) if first == "y" else (qq % 4, pp % 4)
            return src.at[g, yy, xx]

        info.append((p, q, first, second, blk))

    def push(sems, key, src, dst, axis, pos):
        send, recv = sems
        cp = rcopy(src, dst, send.at[key], recv.at[key], plane(axis, pos, j))
        cp.start()
        cps.append(cp)
        return cp

    def add2(dst, b, c):
        for g in range(4):
            dst[g] = (b[g].astype(F32) + c[g].astype(F32)).astype(BF)

    A, B = (asend, arecv), (bsend, brecv)
    av = [dict(), dict()]
    for u in order:
        for a in range(2):
            p, q, first, second, blk = info[a]
            av[a][u, 0] = push(A, (a, u, 0), blk(p + 2, q + u, lo), l1.at[a, u], first, p + 1)
            av[a][u, 1] = push(A, (a, u, 1), blk(p + 2, q + u, hi), r1.at[a, u], first, p + 3)
            av[a][u, 2] = push(A, (a, u, 2), blk(p + 1, q + u, hi), l2.at[a, u, hi], first, p + 1)
            av[a][u, 3] = push(A, (a, u, 3), blk(p + 3, q + u, lo), r2.at[a, u, lo], first, p + 3)
    for u in order:
        for a in range(2):
            p, q, first, second, blk = info[a]
            av[a][u, 0].wait_recv()
            add2(s1.at[a, u], l1.at[a, u], blk(p + 1, q + u, lo))
            av[a][u, 4] = push(A, (a, u, 4), s1.at[a, u], l2.at[a, u, lo], first, p + 1)
            av[a][u, 1].wait_recv()
            add2(s2.at[a, u], r1.at[a, u], blk(p + 3, q + u, hi))
            av[a][u, 5] = push(A, (a, u, 5), s2.at[a, u], r2.at[a, u, hi], first, p + 3)
    bv = [dict(), dict()]
    for u in order:
        for a in range(2):
            p, q, first, second, blk = info[a]
            for i in (2, 3, 4, 5):
                av[a][u, i].wait_recv()
            mine = blk(p, q + u, pl.ds(0, 8))
            for g in range(8):
                acc[a, u, g] = (mine[g].astype(F32) + l2[a, u, g].astype(F32)
                                + r2[a, u, g].astype(F32)).astype(BF)
            if u == 2:
                bv[a][0] = push(B, (a, 0), acc.at[a, 2, lo], bl1.at[a], second, q + 1)
                bv[a][1] = push(B, (a, 1), acc.at[a, 2, hi], br1.at[a], second, q + 3)
            elif u == 1:
                bv[a][2] = push(B, (a, 2), acc.at[a, 1, hi], bl2.at[a, hi], second, q + 1)
            elif u == 3:
                bv[a][3] = push(B, (a, 3), acc.at[a, 3, lo], br2.at[a, lo], second, q + 3)
    for a in range(2):
        p, q, first, second, blk = info[a]
        bv[a][0].wait_recv()
        add2(bs1.at[a], bl1.at[a], acc.at[a, 1, lo])
        bv[a][4] = push(B, (a, 4), bs1.at[a], bl2.at[a, lo], second, q + 1)
        bv[a][1].wait_recv()
        add2(bs2.at[a], br1.at[a], acc.at[a, 3, hi])
        bv[a][5] = push(B, (a, 5), bs2.at[a], br2.at[a, hi], second, q + 3)
    pv = []
    for a in range(2):
        for i in (2, 3, 4, 5):
            bv[a][i].wait_recv()
        for g in range(8):
            fin[a, g] = (acc[a, 0, g].astype(F32) + bl2[a, g].astype(F32)
                         + br2[a, g].astype(F32)).astype(BF)
        for k in range(1, 8):
            g = (d + k) % 8
            cp = rcopy(fin.at[a, g], rec.at[a, d], psend.at[a, k - 1], precv.at[a, k - 1], {"dp": g})
            cp.start()
            cps.append(cp)
            pv.append(cp)
        rec[a, d] = fin[a, d]
    for cp in pv:
        cp.wait_recv()
    rw = rw_ref[...]
    total = jnp.zeros((OWN, 1), F32)
    for k in range(8):
        cols = slice(k * DS, (k + 1) * DS)
        comb = rec[0, k].astype(F32)
        out_o[:, cols] = (rw * comb).astype(BF)
        total = total + jnp.sum(oc_ref[:, cols].astype(F32) * comb, axis=1, keepdims=True)
        out_g[:, cols] = rec[1, k]
    out_w[...] = total
    for cp in cps:
        cp.wait_send()


def reduce_rows(o, g, rw, oc):
    vm = pl.BlockSpec(memory_space=pltpu.VMEM)
    s = jax.ShapeDtypeStruct
    v = lambda *sh: pltpu.VMEM(sh + (OWN, DS), BF)
    dma = lambda *n: pltpu.SemaphoreType.DMA(n)
    return pl.pallas_call(
        reduce_kernel,
        out_shape=(s((OWN, DM), BF), s((OWN, 1), F32), s((OWN, DM), BF)),
        in_specs=[vm] * 4,
        out_specs=(vm,) * 3,
        scratch_shapes=[
            v(2, 4, 4), v(2, 4, 4), v(2, 4, 4), v(2, 4, 4), v(2, 4, 8), v(2, 4, 8), v(2, 4, 8),
            v(2, 4), v(2, 4), v(2, 4), v(2, 4), v(2, 8), v(2, 8), v(2, 8), v(2, 8),
            dma(2, 4, 6), dma(2, 4, 6), dma(2, 6), dma(2, 6), dma(2, 7), dma(2, 7),
        ],
        compiler_params=pltpu.CompilerParams(
            collective_id=1, has_side_effects=True, vmem_limit_bytes=VLIM),
        name="reduce_rows",
    )(o.reshape(GROUPS, 4, 4, OWN, DS), g.reshape(GROUPS, 4, 4, OWN, DS), rw, oc)


def per_device(routed_rows, out_cotangent, route_weight, expert_counts, w_gate, w_up, w_down):
    rw = route_weight[:, None]
    scaled = (rw * out_cotangent.astype(F32)).astype(BF)
    tiles = jnp.sum((expert_counts + 15) // 16, axis=0)
    live = jnp.sum((tiles * 16 + BR - 1) // BR) * BR
    level = sum((live > r).astype(jnp.int32) for r in LEVELS[:-1])
    xg, sg = gather_rows(routed_rows, scaled)
    part, xc, sc = first_matmuls(expert_counts, xg.reshape(ROWS, DS), sg.reshape(ROWS, DS),
                                 w_gate, w_up, w_down)
    h = lax.switch(level, [functools.partial(exchange, r, 2 + i) for i, r in enumerate(LEVELS)], part)
    o, gr, dg, du, dd = second_matmuls(expert_counts, h, xc, sc, w_gate, w_up, w_down)
    layer_out, grad_weight, grad_rows = reduce_rows(o, gr, rw, out_cotangent)
    return (layer_out, grad_weight[:, 0], grad_rows, dg, du, dd)


def solution(mesh):
    return jax.shard_map(
        per_device,
        mesh=mesh,
        in_specs=(
            P(("dp", "et"), None),
            P(("dp", "et"), None),
            P(("dp", "et")),
            P(),
            P(None, None, "et"),
            P(None, None, "et"),
            P(None, "et", None),
        ),
        out_specs=(
            P(("dp", "et"), None),
            P(("dp", "et")),
            P(("dp", "et"), None),
            P(None, "dp", "et"),
            P(None, "dp", "et"),
            P(None, "et", "dp"),
        ),
        check_vma=False,
    )
```

time: 655 us -> 242 us (0.37)
  waiting for transfers between devices: 383 us -> 0 us
  Pallas kernels: 0 us -> 206 us
  matrix products: 152 us -> 0 us
  other arithmetic: 35.4 us -> 3.88 us
  local copies, waits for them, and re-layouts: 53.3 us -> 30.5 us
  loops' own time: 15.9 us -> 0.03 us
  between operations: 14.2 us -> 1.37 us
    reduce_scatter x5 -> x0, waiting for transfers between devices: 274 us -> none  [the longest x1 75.7 us: per_device(): lax.psum_scatter(share_all.astype(jnp.bfloat16), 'et', scatter_dimension=...]
    pallas_call x0 -> x5, Pallas kernels: none -> 206 us  [the longest x1 60.7 us: gather_rows(): pl.pallas_call(gather_kernel, out_shape=(shape, shape), in_specs=[pl.Bloc...]
    dot_general x36 -> x0, matrix products: 152 us -> none  [the longest x12 70.3 us: contract_rows(): lax.dot_general(left, right, (((0,), (0,)), ((), ())), preferred_element_...]
    all_gather x2 -> x0, waiting for transfers between devices: 108 us -> none  [the longest x1 55.6 us: per_device(): gathered = lax.all_gather(routed_rows, 'et', axis=0, tiled=True)]
    unnamed x6 -> x15, local copies, waits for them, and re-layouts: 0.01 us -> 29.8 us
    convert_element_type x4 -> x1, other arithmetic: 30.8 us -> 1.77 us  [per_device(): scaled = (rw * out_cotangent.astype(F32)).astype(BF)]
    while x48 -> x0, local copies, waits for them, and re-layouts: 22.3 us -> none
    another operation x6 -> x0, local copies, waits for them, and re-layouts: 19.2 us -> none
  transfers between devices with their start and end apart: 7 -> 0, of which waited for: 7 -> 0; matrix products, arithmetic and copies ran while one was open for 5% -> 0% of each run, Pallas kernels for 0% -> 0%
where the time goes in v1:
time: 242 us
  Pallas kernels  206 us (85%)
  local copies, waits for them, and re-layouts  30.5 us (13%)
  other arithmetic  3.88 us (2%)
    pallas_call x1, Pallas kernels, gather_rows(): pl.pallas_call(gather_kernel, out_shape=(shape, shape), in_specs=[pl.Bloc...  60.7 us
    pallas_call x1, Pallas kernels, reduce_rows(): pl.pallas_call(reduce_kernel, out_shape=(s((OWN, DM), BF), s((OWN, 1), F3...  60.2 us
    pallas_call x1, Pallas kernels, exchange(): pl.pallas_call(functools.partial(exchange_kernel, r), out_shape=jax.Shape...  58.1 us
    unnamed x15, local copies, waits for them, and re-layouts  29.8 us
    pallas_call x1, Pallas kernels, second_matmuls(): pl.pallas_call(second_kernel, out_shape=(s((ROWS, DS), BF), s((ROWS, DS),...  16.7 us
    pallas_call x1, Pallas kernels, first_matmuls(): pl.pallas_call(first_kernel, out_shape=(jax.ShapeDtypeStruct((3, RMAX, HI...  10.2 us

profile of v1, /device:TPU:1, one launch (start us, length us, event | category | flops | bytes accessed | tf_op | source)
XLA Modules:
  0.0 241.6 jit_solution(917885013125692414)
XLA Ops:
  0.6 1.8 multiply_convert_fusion.sc_ref
  2.4 60.7 %gather_rows.1 = (bf16[8,4,4,32,512]{4,3,2,1,0:T(8,128)(2,1)}, bf16[8,4,4,32,512]{4,3,2,1,0:T(8,128)(2,1)}) custom-call(bf16[32,4096]{1,0:T(8,128)(2,1)} %rows_ref.1, bf16[32,4096]{1,0:T(8,128)(2,1)} %multiply_convert_fusion.sc_ref), custom_call_target="tpu_custom_call" | custom-call | tf_op jit(solution)/shard_map/gather_rows/pallas_call | solution.py:126
  63.1 11.6 %copy.23.wg = bf16[2,4096,448]{2,1,0:T(8,128)(2,1)} copy(bf16[2,4096,448]{1,2,0:T(8,128)(2,1)} %param.15) | data formatting | bytes 14680064 | tf_op args[4]
  74.7 0.0 copy-start.3
  74.7 11.6 %copy.24.wu = bf16[2,4096,448]{2,1,0:T(8,128)(2,1)} copy(bf16[2,4096,448]{1,2,0:T(8,128)(2,1)} %param.16) | data formatting | bytes 14680064 | tf_op args[5]
  86.3 0.0 copy-done.3
  86.3 0.7 copy.25.cnt
  87.0 10.2 %first_matmuls.1 = (bf16[3,4352,448]{2,1,0:T(8,128)(2,1)}, bf16[4352,512]{1,0:T(8,128)(2,1)}, bf16[4352,512]{1,0:T(8,128)(2,1)}) custom-call(s32[8,2]{1,0:T(8,128)} %copy.25.cnt, bf16[4096,512]{1,0:T(8,128)(2,1)} %bitcast.5, bf16[4096,512]{1,0:T(8,128)(2,1)} %bitcast.6, bf16[2,4096,448]{2,1,0:T(8,128)(2,1)} %copy.23.wg, bf16[2,4096,448]{2,1,0:T(8,128)(2,1)} %copy.24.wu, ...), custom_call_target="tpu_custom_call" | custom-call | tf_op jit(solution)/shard_map/first_matmuls/pallas_call | solution.py:254
  97.2 0.1 fusion
  97.3 0.6 fusion.1
  98.6 58.1 %conditional.1 = (bf16[3,4352,448]{2,1,0:T(8,128)(2,1)}) conditional(s32[]{:T(128)} %clamp.3, bf16[3,4352,448]{2,1,0:T(8,128)(2,1)} %get-tuple-element.30, bf16[3,4352,448]{2,1,0:T(8,128)(2,1)} %get-tuple-element.30, bf16[3,4352,448]{2,1,0:T(8,128)(2,1)} %get-tuple-element.30, ...), branch_computations={%region_2.3_spmd, %region_3.4_spmd, %region_4.5_spmd, %region_5.6_... | conditional | bytes 8 | solution.py:627
  98.6 58.1 %exchange_1792.1 = bf16[3,4352,448]{2,1,0:T(8,128)(2,1)} custom-call(bf16[3,4352,448]{2,1,0:T(8,128)(2,1)} %p.1), custom_call_target="tpu_custom_call" | custom-call | tf_op jit(solution)/shard_map/cond/branch_1_fun/exchange_1792/pallas_call | solution.py:377
  156.8 0.0 copy-start.2
  156.8 16.7 %second_matmuls.1 = (bf16[4096,512]{1,0:T(8,128)(2,1)}, bf16[4096,512]{1,0:T(8,128)(2,1)}, bf16[2,512,448]{2,1,0:T(8,128)(2,1)}, bf16[2,512,448]{2,1,0:T(8,128)(2,1)}, bf16[2,448,512]{2,1,0:T(8,128)(2,1)}) custom-call(s32[8,2]{1,0:T(8,128)} %copy.25.cnt, bf16[3,4352,448]{2,1,0:T(8,128)(2,1)} %get-tuple-element.65.h, ...), custom_call_target="tpu_custom_call" | custom-call | tf_op jit(solution)/shard_map/second_matmuls/pallas_call | solution.py:474
  173.5 0.0 copy-start.1
  173.5 0.0 copy-start
  173.5 0.0 copy-done.2
  173.5 0.7 copy.28.rw_ref
  174.2 60.2 %reduce_rows.1 = (bf16[32,4096]{1,0:T(8,128)(2,1)}, f32[32,1]{1,0:T(8,128)}, bf16[32,4096]{1,0:T(8,128)(2,1)}) custom-call(bf16[8,4,4,32,512]{4,3,2,1,0:T(8,128)(2,1)} %bitcast.7, bf16[8,4,4,32,512]{4,3,2,1,0:T(8,128)(2,1)} %bitcast.8, f32[32,1]{1,0:T(8,128)} %copy.28.rw_ref, bf16[32,4096]{1,0:T(8,128)(2,1)} %oc_ref.1), custom_call_target="tpu_custom_call" | custom-call | tf_op jit(solution)/shard_map/reduce_rows/pallas_call | solution.py:602
  234.4 1.3 reduce
  235.7 0.0 copy-done.1
  235.7 1.3 copy.29
  237.0 0.0 copy-done
  237.0 1.3 copy.30
  238.2 1.7 copy.37
  239.9 1.7 copy.38
Async XLA Ops:
  74.7 11.6 %copy-start.3 = (s32[8,2]{0,1:T(2,128)S(1)}, s32[8,2]{0,1:T(2,128)}, u32[]{:S(2)}) copy-start(s32[8,2]{0,1:T(2,128)} %param.14) | copy-start | bytes 196
  156.8 16.7 %copy-start.2 = (f32[32]{0:T(128)S(1)}, f32[32]{0:T(128)}, u32[]{:S(2)}) copy-start(f32[32]{0:T(128)} %param.13) | copy-start | bytes 388
  173.5 62.2 %copy-start.1 = (bf16[2,512,448]{2,1,0:T(8,128)(2,1)S(1)}, bf16[2,512,448]{2,1,0:T(8,128)(2,1)}, u32[]{:S(2)}) copy-start(bf16[2,512,448]{2,1,0:T(8,128)(2,1)} %get-tuple-element.50) | copy-start | bytes 2752516
  173.5 63.5 %copy-start = (bf16[2,512,448]{2,1,0:T(8,128)(2,1)S(1)}, bf16[2,512,448]{2,1,0:T(8,128)(2,1)}, u32[]{:S(2)}) copy-start(bf16[2,512,448]{2,1,0:T(8,128)(2,1)} %get-tuple-element.51) | copy-start | bytes 2752516

commit v2 on v1

v2 whole, which is shorter than its diff:
```python
import functools

import jax
import jax.numpy as jnp
from jax import lax
from jax.experimental import pallas as pl
from jax.experimental.pallas import tpu as pltpu
from jax.sharding import PartitionSpec as P

MESH = pl.DeviceIdType.MESH
BF = jnp.bfloat16
F32 = jnp.float32
GROUPS, SLOTS, OWN, DM, HID = 8, 512, 32, 4096, 448
DS = DM // GROUPS
ROWS = GROUPS * SLOTS
H2, H3 = 2 * HID, 3 * HID
BR = 256
T = 16
TB = BR // T
PLANS = ((8, (1536, 1792, 2304)), (10, (2816,)), (16, (ROWS + BR,)))
VLIM = 60 * 1024 * 1024


def rcopy(src, dst, ssem, rsem, dev):
    return pltpu.make_async_remote_copy(
        src_ref=src, dst_ref=dst, send_sem=ssem, recv_sem=rsem,
        device_id=dev, device_id_type=MESH,
    )


def spot(g, s):
    return (s + 3 * g + 8 * (s // 16)) % 16


def origin(g, m, j):
    return 16 * m + (j + 32 - 3 * g - 8 * m) % 16


def plane(axis, pos, j):
    y, x = j // 4, j % 4
    return {"et": y * 4 + pos % 4} if axis == "x" else {"et": (pos % 4) * 4 + x}


def greet(near, others):
    bar = pltpu.get_barrier_semaphore()
    for dev in near:
        pl.semaphore_signal(bar, inc=1, device_id=dev, device_id_type=MESH)
    for dd, jj in others:
        pl.semaphore_signal(bar, inc=1, device_id={"dp": dd, "et": jj}, device_id_type=MESH)
    pl.semaphore_wait(bar, len(near) + len(others))


def deliver(me, src, dst, ssem, rsem, dd, jj):
    d, j = me
    here = jnp.logical_and(dd == d, jj == j)
    far = rcopy(src, dst, ssem, rsem, {"dp": dd, "et": jj})

    @pl.when(here)
    def _():
        pltpu.make_async_copy(src, dst, rsem).start()

    @pl.when(jnp.logical_not(here))
    def _():
        far.start()

    def finish():
        @pl.when(jnp.logical_not(here))
        def _():
            far.wait_send()

    return finish


def gather_kernel(cap, tab, rows_ref, oc_ref, rw_ref, xg, sg,
                  sc, rb0, rb1, stage, psend, precv, osem, rsend, rrecv):
    d, j = lax.axis_index("dp"), lax.axis_index("et")
    me = (d, j)
    y, x = j // 4, j % 4
    lo = cap // 2
    senders = [((d + 8 - k) % 8, origin((d + 8 - k) % 8, m, j) // 2) for k in range(8) for m in range(2)]
    greet([plane("x", x + 1, j), plane("x", x + 3, j), plane("y", y + 1, j), plane("y", y + 3, j)],
          senders)
    mm = j // 8
    rb = (rb0, rb1)
    done = []
    arrays = []
    for a, (src, out, first, second) in enumerate(
        ((rows_ref, xg, "x", "y"), (sc, sg, "y", "x"))
    ):
        if a == 1:
            sc[...] = (rw_ref[...] * oc_ref[...].astype(F32)).astype(BF)
        for k in range(8):
            dd = (d + k) % 8
            cols = pl.ds(pl.multiple_of(dd * DS, DS), DS)
            for hh in range(2):
                jj = spot(d, 2 * j + hh)
                done.append(deliver(me, src.at[pl.ds(T * hh, T), cols], rb[a].at[2 * d + mm],
                                    psend.at[a, k, hh], precv.at[a, k, mm], dd, jj))
        p, q = (x, y) if first == "x" else (y, x)

        def blk(pp, qq, half=None, out=out, first=first):
            yy, xx = (qq % 4, pp % 4) if first == "x" else (pp % 4, qq % 4)
            g = slice(None) if half is None else (pl.ds(0, lo) if half == 0 else pl.ds(lo, cap - lo))
            return out.at[yy, xx, g]

        def send(i, ref, axis, pos, a=a, own=None):
            c = rcopy(ref if own is None else own, ref, rsend.at[a, i], rrecv.at[a, i], plane(axis, pos, j))
            c.start()
            return c

        arrays.append((p, q, first, second, blk, send))

    sent = [dict(), dict()]

    def second_sends(a, u, own=None):
        p, q, first, second, blk, send = arrays[a]
        base = 4 + 4 * (u % 4)
        sent[a][base] = send(base, blk(p + u, q), second, q + 1, own=own)
        sent[a][base + 1] = send(base + 1, blk(p + u, q), second, q + 3, own=own)

    def second_forward(a, u):
        p, q, first, second, blk, send = arrays[a]
        base = 4 + 4 * (u % 4)
        sent[a][base].wait_recv()
        sent[a][base + 2] = send(base + 2, blk(p + u, q + 3, 0), second, q + 1)
        sent[a][base + 1].wait_recv()
        sent[a][base + 3] = send(base + 3, blk(p + u, q + 1, 1), second, q + 3)

    keep = []
    for a in range(2):
        p, q, first, second, blk, send = arrays[a]
        for k in range(8):
            for m in range(2):
                g = (d + 8 - k) % 8
                pltpu.make_async_copy(rb[a].at[2 * g + m], rb[a].at[2 * g + m], precv.at[a, k, m]).wait()
        for i in range(cap):
            stage[a, i] = rb[a][tab[j, i]]
        sent[a][0] = send(0, blk(p, q), first, p + 1, own=stage.at[a])
        sent[a][1] = send(1, blk(p, q), first, p + 3, own=stage.at[a])
        second_sends(a, 0, own=stage.at[a])
        c = pltpu.make_async_copy(stage.at[a], blk(p, q), osem.at[a])
        c.start()
        keep.append(c)
    for a in range(2):
        p, q, first, second, blk, send = arrays[a]
        sent[a][0].wait_recv()
        sent[a][2] = send(2, blk(p + 3, q, 0), first, p + 1)
        second_sends(a, 3)
        sent[a][1].wait_recv()
        sent[a][3] = send(3, blk(p + 1, q, 1), first, p + 3)
        second_sends(a, 1)
    for a in range(2):
        second_forward(a, 0)
    for a in range(2):
        sent[a][2].wait_recv()
        sent[a][3].wait_recv()
        second_sends(a, 2)
    for u in (3, 1, 2):
        for a in range(2):
            second_forward(a, u)
    for a in range(2):
        keep[a].wait()
        for u in range(4):
            sent[a][6 + 4 * u].wait_recv()
            sent[a][7 + 4 * u].wait_recv()
        for c in sent[a].values():
            c.wait_send()
    for f in done:
        f()


def gather_rows(cap, cid, tab, rows, oc, rw):
    shape = jax.ShapeDtypeStruct((4, 4, cap, T, DS), BF)
    vm = pl.BlockSpec(memory_space=pltpu.VMEM)
    return pl.pallas_call(
        functools.partial(gather_kernel, cap),
        out_shape=(shape, shape),
        in_specs=[pl.BlockSpec(memory_space=pltpu.SMEM), vm, vm, vm],
        out_specs=(pl.BlockSpec(memory_space=pl.ANY),) * 2,
        scratch_shapes=[
            pltpu.VMEM((OWN, DM), BF),
            pltpu.VMEM((16, T, DS), BF),
            pltpu.VMEM((16, T, DS), BF),
            pltpu.VMEM((2, cap, T, DS), BF),
            pltpu.SemaphoreType.DMA((2, 8, 2)),
            pltpu.SemaphoreType.DMA((2, 8, 2)),
            pltpu.SemaphoreType.DMA((2,)),
            pltpu.SemaphoreType.DMA((2, 20)),
            pltpu.SemaphoreType.DMA((2, 20)),
        ],
        compiler_params=pltpu.CompilerParams(
            collective_id=cid, has_side_effects=True, vmem_limit_bytes=VLIM),
        name="gather_rows_%d" % cap,
    )(tab, rows, oc, rw)


def segments(cnt):
    segs, t = [], 0
    ends = []
    for e in range(2):
        row = []
        for g in range(GROUPS):
            c = cnt[g, e]
            first = 0 if e == 0 else (cnt[g, 0] + 127) // 128 * 8
            n = (c + T - 1) // T
            row.append((c, first, n, t))
            t = t + n
        ends.append(t)
        t = (t + TB - 1) // TB * TB
        ends.append(t)
        segs.append(row)
    return segs, ends


def tile(i):
    return pl.ds(pl.multiple_of(i * T, T), T)


def rows_of(b):
    return pl.ds(pl.multiple_of(b * BR, BR), BR)


def weight_copies(wg, wu, wd, wb, wsem):
    d = lax.axis_index("dp")
    cols = pl.ds(pl.multiple_of(d * DS, DS), DS)
    return [pltpu.make_async_copy(w.at[:, :, cols], wb.at[:, pl.ds(i * HID, HID), :], wsem.at[i])
            for i, w in enumerate((wg, wu, wd))]


TRANS_R = (((1,), (1,)), ((), ()))
TRANS_L = (((0,), (0,)), ((), ()))


def first_kernel(cap, cnt, tab, xg, sg, wg, wu, wd, part, xc_o, sc_o,
                 xv, sv, xc, sc, wb, pv, rsem, wsem, osem):
    segs, ends = segments(cnt)
    loads = [pltpu.make_async_copy(xg, xv, rsem.at[0]), pltpu.make_async_copy(sg, sv, rsem.at[1])]
    wcp = weight_copies(wg, wu, wd, wb, wsem)
    for c in loads + wcp:
        c.start()
    for c in loads:
        c.wait()
    zeros = jnp.zeros((T, DS), BF)
    iota = lax.broadcasted_iota(jnp.int32, (T, DS), 0)

    def source(g, s):
        jj = spot(g, s)
        return tile(jj * cap + tab[16 + jj, 2 * g + s // 16])

    for e in range(2):
        for g in range(GROUPS):
            c, first, n, t0 = segs[e][g]

            def move(k, _, g=g, first=first, t0=t0):
                src = source(g, first + k)
                xc[tile(t0 + k), :] = xv[src, :]
                sc[tile(t0 + k), :] = sv[src, :]
                return 0

            lax.fori_loop(0, n - 1, move, 0)
            keep = iota < c - T * (n - 1)
            src = source(g, first + n - 1)
            xt = xv[src, :].astype(F32)
            st = sv[src, :].astype(F32)
            xc[tile(t0 + n - 1), :] = jnp.where(keep, xt, 0.0).astype(BF)
            sc[tile(t0 + n - 1), :] = jnp.where(keep, st, 0.0).astype(BF)

        def blank(t, _):
            xc[tile(t), :] = zeros
            sc[tile(t), :] = zeros
            return 0

        lax.fori_loop(ends[2 * e], ends[2 * e + 1], blank, 0)
    for c in wcp:
        c.wait()
    nb0, nb = ends[1] // TB, ends[3] // TB

    def out_copies(b):
        rows = rows_of(b)
        return (pltpu.make_async_copy(pv.at[rows], part.at[rows], osem.at[0]),
                pltpu.make_async_copy(xc.at[rows], xc_o.at[rows], osem.at[1]),
                pltpu.make_async_copy(sc.at[rows], sc_o.at[rows], osem.at[2]))

    def block(b, _):
        e = (b >= nb0).astype(jnp.int32)
        rows = rows_of(b)
        pv[rows, 0:H2] = lax.dot_general(
            xc[rows, :], wb[e, 0:H2, :], TRANS_R, preferred_element_type=F32).astype(BF)
        pv[rows, H2:H3] = lax.dot_general(
            sc[rows, :], wb[e, H2:H3, :], TRANS_R, preferred_element_type=F32).astype(BF)
        for c in out_copies(b):
            c.start()
        return 0

    lax.fori_loop(0, nb, block, 0)

    def drain(b, _):
        for c in out_copies(b):
            c.wait()
        return 0

    lax.fori_loop(0, nb, drain, 0)


def first_matmuls(cap, rmax, counts, tab, xg, sg, wg, wu, wd):
    any_ = pl.BlockSpec(memory_space=pl.ANY)
    sm = pl.BlockSpec(memory_space=pltpu.SMEM)
    n = 16 * cap * T
    return pl.pallas_call(
        functools.partial(first_kernel, cap),
        out_shape=(jax.ShapeDtypeStruct((rmax, H3), BF),
                   jax.ShapeDtypeStruct((rmax, DS), BF),
                   jax.ShapeDtypeStruct((rmax, DS), BF)),
        in_specs=[sm, sm] + [any_] * 5,
        out_specs=(any_,) * 3,
        scratch_shapes=[
            pltpu.VMEM((n, DS), BF), pltpu.VMEM((n, DS), BF),
            pltpu.VMEM((rmax, DS), BF), pltpu.VMEM((rmax, DS), BF),
            pltpu.VMEM((2, H3, DS), BF),
            pltpu.VMEM((rmax, H3), BF),
            pltpu.SemaphoreType.DMA((2,)), pltpu.SemaphoreType.DMA((3,)),
            pltpu.SemaphoreType.DMA((3,)),
        ],
        compiler_params=pltpu.CompilerParams(vmem_limit_bytes=VLIM),
        name="first_matmuls_%d" % cap,
    )(counts, tab, xg.reshape(n, DS), sg.reshape(n, DS), wg, wu, wd)


def exchange_kernel(r, p, h, own, prt, q, l1, r1, s1, s2, l2, r2, tot, res,
                    osem, psend, precv, bsend, brecv, gsend, grecv, lsem):
    d = lax.axis_index("dp")
    z, c = d // 2, d % 2
    r8, r16 = r // 8, r // 16
    up, down = {"dp": (z + 1) % 4 * 2 + c}, {"dp": (z + 3) % 4 * 2 + c}
    mate = {"dp": z * 2 + 1 - c}
    bar = pltpu.get_barrier_semaphore()
    for dev in (up, down, mate):
        pl.semaphore_signal(bar, inc=1, device_id=dev, device_id_type=MESH)
    pl.semaphore_wait(bar, 3)

    def rows(zz, cc):
        return pl.ds(pl.multiple_of((zz % 4 * 2 + cc) * r8, r16), r8)

    def half(zz, cc, i):
        return pl.ds(pl.multiple_of((zz % 4 * 2 + cc) * r8 + i * r16, r16), r16)

    first, second = pl.ds(0, r16), pl.ds(r16, r16)
    pair, mine = {}, {}
    for i in (2, 1, 3, 0):
        pair[i] = rcopy(p.at[rows(z + i, 1 - c)], prt.at[i], psend.at[i], precv.at[i], mate)
        pair[i].start()
        mine[i] = pltpu.make_async_copy(p.at[rows(z + i, c)], own.at[i], osem.at[i])
        mine[i].start()

    def bsum(i):
        mine[i].wait()
        pair[i].wait_recv()

        def one(k, _):
            q[i, tile(k), :] = (own[i, tile(k), :].astype(F32) + prt[i, tile(k), :].astype(F32)).astype(BF)
            return 0

        lax.fori_loop(0, r8 // T, one, 0)

    def add_rows(dst, src, i, off):
        def one(k, _):
            dst[tile(k), :] = (src[tile(k), :].astype(F32) + q[i, tile(off + k), :].astype(F32)).astype(BF)
            return 0

        lax.fori_loop(0, r16 // T, one, 0)

    cps = []

    def push(i, src, dst, dev):
        cp = rcopy(src, dst, bsend.at[i], brecv.at[i], dev)
        cp.start()
        cps.append(cp)
        return cp

    bsum(2)
    a_l = push(0, q.at[2, first], l1, up)
    a_r = push(1, q.at[2, second], r1, down)
    bsum(1)
    b_l2 = push(2, q.at[1, second], l2.at[second], up)
    bsum(3)
    b_r1 = push(3, q.at[3, first], r2.at[first], down)
    a_l.wait_recv()
    add_rows(s1, l1, 1, 0)
    b_l1 = push(4, s1, l2.at[first], up)
    a_r.wait_recv()
    add_rows(s2, r1, 3, r16 // T)
    b_r2 = push(5, s2, r2.at[second], down)
    mine[0].wait()
    pair[0].wait_recv()
    for cp in (b_l2, b_r1, b_l1, b_r2):
        cp.wait_recv()

    def final(k, _):
        t = tile(k)
        tot[...] = (own[0, t, :].astype(F32) + prt[0, t, :].astype(F32)
                    + l2[t, :].astype(F32) + r2[t, :].astype(F32))
        gate, lin, grad = tot[:, 0:HID], tot[:, HID:H2], tot[:, H2:H3]
        s = 1.0 / (1.0 + jnp.exp(-gate))
        act = gate * s
        res[t, 0:HID] = (grad * lin * s * (1.0 + gate * (1.0 - s))).astype(BF)
        res[t, HID:H2] = (grad * act).astype(BF)
        res[t, H2:H3] = (act * lin).astype(BF)
        return 0

    lax.fori_loop(0, r8 // T, final, 0)
    keep = pltpu.make_async_copy(res, h.at[rows(z, c)], lsem)
    keep.start()
    gps = {}

    def spread(i, src, dst, dev):
        cp = rcopy(src, dst, gsend.at[i], grecv.at[i], dev)
        cp.start()
        gps[i] = cp

    spread(0, res, h.at[rows(z, c)], up)
    spread(1, res, h.at[rows(z, c)], down)
    spread(2, res, h.at[rows(z, c)], mate)
    gps[0].wait_recv()
    spread(3, h.at[half(z + 3, c, 0)], h.at[half(z + 3, c, 0)], up)
    spread(4, h.at[rows(z + 3, c)], h.at[rows(z + 3, c)], mate)
    gps[1].wait_recv()
    spread(5, h.at[half(z + 1, c, 1)], h.at[half(z + 1, c, 1)], down)
    spread(6, h.at[rows(z + 1, c)], h.at[rows(z + 1, c)], mate)
    gps[3].wait_recv()
    spread(7, h.at[half(z + 2, c, 0)], h.at[half(z + 2, c, 0)], mate)
    gps[5].wait_recv()
    spread(8, h.at[half(z + 2, c, 1)], h.at[half(z + 2, c, 1)], mate)
    for i in (2, 4, 6, 7, 8):
        gps[i].wait_recv()
    keep.wait()
    for cp in list(pair.values()) + cps + list(gps.values()):
        cp.wait_send()


def exchange(r, rmax, cid, part):
    r8, r16 = r // 8, r // 16
    any_ = pl.BlockSpec(memory_space=pl.ANY)
    v = lambda *s: pltpu.VMEM(s + (H3,), BF)
    dma = lambda n: pltpu.SemaphoreType.DMA((n,))
    return pl.pallas_call(
        functools.partial(exchange_kernel, r),
        out_shape=jax.ShapeDtypeStruct((rmax, H3), BF),
        in_specs=[any_],
        out_specs=any_,
        scratch_shapes=[
            v(4, r8), v(4, r8), v(4, r8),
            v(r16), v(r16), v(r16), v(r16),
            v(r8), v(r8), pltpu.VMEM((T, H3), F32), v(r8),
            dma(4), dma(4), dma(4), dma(6), dma(6), dma(9), dma(9), pltpu.SemaphoreType.DMA,
        ],
        compiler_params=pltpu.CompilerParams(
            collective_id=cid, has_side_effects=True, vmem_limit_bytes=VLIM),
        name="exchange_%d_%d" % (cid, r),
    )(part)


def second_kernel(cap, cnt, tab, h, xc_i, sc_i, wg, wu, wd, o, gr, dg, du, dd,
                  hv, xc, sc, wb, ov, gv, au, ad, bsem, wsem):
    segs, ends = segments(cnt)
    nb0, nb = ends[1] // TB, ends[3] // TB
    wcp = weight_copies(wg, wu, wd, wb, wsem)

    def in_copies(b):
        rows = rows_of(b)
        return (pltpu.make_async_copy(h.at[rows], hv.at[rows], bsem.at[0, b]),
                pltpu.make_async_copy(xc_i.at[rows], xc.at[rows], bsem.at[1, b]),
                pltpu.make_async_copy(sc_i.at[rows], sc.at[rows], bsem.at[2, b]))

    for c in wcp:
        c.start()

    def begin(b, _):
        for c in in_copies(b):
            c.start()
        return 0

    lax.fori_loop(0, nb, begin, 0)
    au[...] = jnp.zeros_like(au)
    ad[...] = jnp.zeros_like(ad)
    for c in wcp:
        c.wait()

    def block(b, _):
        e = (b >= nb0).astype(jnp.int32)
        rows = rows_of(b)
        for c in in_copies(b):
            c.wait()
        ov[rows, :] = jnp.dot(hv[rows, H2:H3], wb[e, H2:H3, :], preferred_element_type=F32).astype(BF)
        gv[rows, :] = jnp.dot(hv[rows, 0:H2], wb[e, 0:H2, :], preferred_element_type=F32).astype(BF)
        au[e] += lax.dot_general(hv[rows, 0:H2], xc[rows, :], TRANS_L, preferred_element_type=F32)
        ad[e] += lax.dot_general(hv[rows, H2:H3], sc[rows, :], TRANS_L, preferred_element_type=F32)
        return 0

    lax.fori_loop(0, nb, block, 0)
    dg[...] = au[:, 0:HID, :].astype(BF)
    du[...] = au[:, HID:H2, :].astype(BF)
    dd[...] = ad[...].astype(BF)

    for e in range(2):
        for g in range(GROUPS):
            c, first, n, t0 = segs[e][g]

            def move(k, _, g=g, first=first, t0=t0):
                s = first + k
                jj = spot(g, s)
                dst = tile(jj * cap + tab[16 + jj, 2 * g + s // 16])
                o[dst, :] = ov[tile(t0 + k), :]
                gr[dst, :] = gv[tile(t0 + k), :]
                return 0

            lax.fori_loop(0, n, move, 0)


def second_matmuls(cap, rmax, counts, tab, h, xc, sc, wg, wu, wd):
    any_ = pl.BlockSpec(memory_space=pl.ANY)
    sm = pl.BlockSpec(memory_space=pltpu.SMEM)
    vm = pl.BlockSpec(memory_space=pltpu.VMEM)
    s = jax.ShapeDtypeStruct
    n = 16 * cap * T
    return pl.pallas_call(
        functools.partial(second_kernel, cap),
        out_shape=(s((n, DS), BF), s((n, DS), BF)) + (s((2, HID, DS), BF),) * 3,
        in_specs=[sm, sm] + [any_] * 6,
        out_specs=(vm,) * 5,
        scratch_shapes=[
            pltpu.VMEM((rmax, H3), BF),
            pltpu.VMEM((rmax, DS), BF), pltpu.VMEM((rmax, DS), BF),
            pltpu.VMEM((2, H3, DS), BF),
            pltpu.VMEM((rmax, DS), BF), pltpu.VMEM((rmax, DS), BF),
            pltpu.VMEM((2, H2, DS), F32), pltpu.VMEM((2, HID, DS), F32),
            pltpu.SemaphoreType.DMA((3, rmax // BR)), pltpu.SemaphoreType.DMA((3,)),
        ],
        compiler_params=pltpu.CompilerParams(vmem_limit_bytes=VLIM),
        name="second_matmuls_%d" % cap,
    )(counts, tab, h, xc, sc, wg, wu, wd)


def reduce_kernel(cap, tab, o_ref, g_ref, rw_ref, oc_ref, out_o, out_w, out_g,
                  l1, r1, s1, s2, l2, r2, acc, bl1, br1, bs1, bs2, bl2, br2, fin, ex, rec,
                  asend, arecv, bsend, brecv, psend, precv):
    d, j = lax.axis_index("dp"), lax.axis_index("et")
    me = (d, j)
    y, x = j // 4, j % 4
    owners = [((d + k) % 8, spot(d, 2 * j + hh)) for k in range(8) for hh in range(2)]
    greet([plane("x", x + 1, j), plane("x", x + 3, j), plane("y", y + 1, j), plane("y", y + 3, j)],
          owners)
    half = cap // 2
    lo, hi = pl.ds(0, half), pl.ds(half, cap - half)
    order = (2, 1, 3, 0)
    info = []
    cps = []
    for a, (src, first) in enumerate(((o_ref, "y"), (g_ref, "x"))):
        second = "x" if first == "y" else "y"
        p, q = (y, x) if first == "y" else (x, y)

        def blk(pp, qq, g, src=src, first=first):
            yy, xx = (pp % 4, qq % 4) if first == "y" else (qq % 4, pp % 4)
            return src.at[yy, xx, g]

        info.append((p, q, first, second, blk))

    def push(sems, key, src, dst, axis, pos):
        send, recv = sems
        cp = rcopy(src, dst, send.at[key], recv.at[key], plane(axis, pos, j))
        cp.start()
        cps.append(cp)
        return cp

    def add2(dst, b, c):
        for g in range(half):
            dst[g] = (b[g].astype(F32) + c[g].astype(F32)).astype(BF)

    A, B = (asend, arecv), (bsend, brecv)
    av = [dict(), dict()]
    for u in order:
        for a in range(2):
            p, q, first, second, blk = info[a]
            av[a][u, 0] = push(A, (a, u, 0), blk(p + 2, q + u, lo), l1.at[a, u], first, p + 1)
            av[a][u, 1] = push(A, (a, u, 1), blk(p + 2, q + u, hi), r1.at[a, u], first, p + 3)
            av[a][u, 2] = push(A, (a, u, 2), blk(p + 1, q + u, hi), l2.at[a, u, hi], first, p + 1)
            av[a][u, 3] = push(A, (a, u, 3), blk(p + 3, q + u, lo), r2.at[a, u, lo], first, p + 3)
    for u in order:
        for a in range(2):
            p, q, first, second, blk = info[a]
            av[a][u, 0].wait_recv()
            add2(s1.at[a, u], l1.at[a, u], blk(p + 1, q + u, lo))
            av[a][u, 4] = push(A, (a, u, 4), s1.at[a, u], l2.at[a, u, lo], first, p + 1)
            av[a][u, 1].wait_recv()
            add2(s2.at[a, u], r1.at[a, u], blk(p + 3, q + u, hi))
            av[a][u, 5] = push(A, (a, u, 5), s2.at[a, u], r2.at[a, u, hi], first, p + 3)
    bv = [dict(), dict()]
    for u in order:
        for a in range(2):
            p, q, first, second, blk = info[a]
            for i in (2, 3, 4, 5):
                av[a][u, i].wait_recv()
            mine = blk(p, q + u, pl.ds(0, cap))
            for g in range(cap):
                acc[a, u, g] = (mine[g].astype(F32) + l2[a, u, g].astype(F32)
                                + r2[a, u, g].astype(F32)).astype(BF)
            if u == 2:
                bv[a][0] = push(B, (a, 0), acc.at[a, 2, lo], bl1.at[a], second, q + 1)
                bv[a][1] = push(B, (a, 1), acc.at[a, 2, hi], br1.at[a], second, q + 3)
            elif u == 1:
                bv[a][2] = push(B, (a, 2), acc.at[a, 1, hi], bl2.at[a, hi], second, q + 1)
            elif u == 3:
                bv[a][3] = push(B, (a, 3), acc.at[a, 3, lo], br2.at[a, lo], second, q + 3)
    for a in range(2):
        p, q, first, second, blk = info[a]
        bv[a][0].wait_recv()
        add2(bs1.at[a], bl1.at[a], acc.at[a, 1, lo])
        bv[a][4] = push(B, (a, 4), bs1.at[a], bl2.at[a, lo], second, q + 1)
        bv[a][1].wait_recv()
        add2(bs2.at[a], br1.at[a], acc.at[a, 3, hi])
        bv[a][5] = push(B, (a, 5), bs2.at[a], br2.at[a, hi], second, q + 3)
    done = []
    for a in range(2):
        for i in (2, 3, 4, 5):
            bv[a][i].wait_recv()
        for g in range(cap):
            fin[a, g] = (acc[a, 0, g].astype(F32) + bl2[a, g].astype(F32)
                         + br2[a, g].astype(F32)).astype(BF)
        for k in range(8):
            g = (d + k) % 8
            for m in range(2):
                s = origin(g, m, j)
                at = tab[16 + j, 2 * g + m]
                got = fin[a, jnp.maximum(at, 0)].astype(F32)
                ex[a, k, m] = jnp.where(at >= 0, got, 0.0).astype(BF)
                done.append(deliver(me, ex.at[a, k, m], rec.at[a, d, s % 2],
                                    psend.at[a, k, m], precv.at[a, k, s % 2], g, s // 2))
    for a in range(2):
        for k in range(8):
            for hh in range(2):
                spot_ref = rec.at[a, (d + 8 - k) % 8, hh]
                pltpu.make_async_copy(spot_ref, spot_ref, precv.at[a, k, hh]).wait()
    rw = rw_ref[...]
    total = jnp.zeros((OWN, 1), F32)
    for k in range(8):
        cols = slice(k * DS, (k + 1) * DS)
        comb = rec[0, k].astype(F32).reshape(OWN, DS)
        out_o[:, cols] = (rw * comb).astype(BF)
        total = total + jnp.sum(oc_ref[:, cols].astype(F32) * comb, axis=1, keepdims=True)
        out_g[:, cols] = rec[1, k].reshape(OWN, DS)
    out_w[...] = total
    for cp in cps:
        cp.wait_send()
    for f in done:
        f()


def reduce_rows(cap, cid, tab, o, g, rw, oc):
    vm = pl.BlockSpec(memory_space=pltpu.VMEM)
    s = jax.ShapeDtypeStruct
    v = lambda *sh: pltpu.VMEM(sh + (T, DS), BF)
    dma = lambda *n: pltpu.SemaphoreType.DMA(n)
    h = cap // 2
    return pl.pallas_call(
        functools.partial(reduce_kernel, cap),
        out_shape=(s((OWN, DM), BF), s((OWN, 1), F32), s((OWN, DM), BF)),
        in_specs=[pl.BlockSpec(memory_space=pltpu.SMEM)] + [vm] * 4,
        out_specs=(vm,) * 3,
        scratch_shapes=[
            v(2, 4, h), v(2, 4, h), v(2, 4, h), v(2, 4, h), v(2, 4, cap), v(2, 4, cap), v(2, 4, cap),
            v(2, h), v(2, h), v(2, h), v(2, h), v(2, cap), v(2, cap), v(2, cap),
            v(2, 8, 2), v(2, 8, 2),
            dma(2, 4, 6), dma(2, 4, 6), dma(2, 6), dma(2, 6), dma(2, 8, 2), dma(2, 8, 2),
        ],
        compiler_params=pltpu.CompilerParams(
            collective_id=cid, has_side_effects=True, vmem_limit_bytes=VLIM),
        name="reduce_rows_%d" % cap,
    )(tab, o.reshape(4, 4, cap, T, DS), g.reshape(4, 4, cap, T, DS), rw, oc)


def tile_tables(counts):
    j = lax.broadcasted_iota(jnp.int32, (16, 16), 0)
    q = lax.broadcasted_iota(jnp.int32, (16, 16), 1)
    g, m = q // 2, q % 2
    s = origin(g, m, j)
    c = jnp.repeat(counts, 2, axis=0)
    n0, n1 = (c[:, 0] + T - 1) // T, (c[:, 1] + T - 1) // T
    s1 = (c[:, 0] + 127) // 128 * 8
    live = (s < n0) | ((s >= s1) & (s < s1 + n1))
    one = live.astype(jnp.int32)
    rank = jnp.sum(jnp.where(q[:, None, :] < q[:, :, None], one[:, None, :], 0), axis=2)
    place = jnp.where(live, rank, -1)
    order = jnp.sum(jnp.where(place[:, None, :] == q[:, :, None], q[:, None, :], 0), axis=2)
    return jnp.concatenate([order, place], axis=0), jnp.max(jnp.sum(one, axis=1))


def run(cap, levels, cid, rows, oc, rw, counts, tab, live, wg, wu, wd):
    rmax = levels[-1]
    xg, sg = gather_rows(cap, cid, tab, rows, oc, rw)
    part, xc, sc = first_matmuls(cap, rmax, counts, tab, xg, sg, wg, wu, wd)
    level = sum((live > r).astype(jnp.int32) for r in levels[:-1])
    h = lax.switch(level, [functools.partial(exchange, r, rmax, cid + 2 + i)
                           for i, r in enumerate(levels)], part)
    o, gr, dg, du, dd = second_matmuls(cap, rmax, counts, tab, h, xc, sc, wg, wu, wd)
    layer_out, grad_weight, grad_rows = reduce_rows(cap, cid + 1, tab, o, gr, rw, oc)
    return layer_out, grad_weight, grad_rows, dg, du, dd


def per_device(routed_rows, out_cotangent, route_weight, expert_counts, w_gate, w_up, w_down):
    rw = route_weight[:, None]
    wg, wu = jnp.swapaxes(w_gate, 1, 2), jnp.swapaxes(w_up, 1, 2)
    tab, most = tile_tables(expert_counts)
    tiles = jnp.sum((expert_counts + T - 1) // T, axis=0)
    live = jnp.sum((tiles + TB - 1) // TB) * BR
    pick = sum((most > cap).astype(jnp.int32) for cap, _ in PLANS[:-1])
    branches = [functools.partial(run, cap, levels, 8 * i) for i, (cap, levels) in enumerate(PLANS)]
    layer_out, grad_weight, grad_rows, dg, du, dd = lax.switch(
        pick, branches, routed_rows, out_cotangent, rw, expert_counts, tab, live, wg, wu, w_down)
    return (layer_out, grad_weight[:, 0], grad_rows,
            jnp.swapaxes(dg, 1, 2), jnp.swapaxes(du, 1, 2), dd)


def solution(mesh):
    return jax.shard_map(
        per_device,
        mesh=mesh,
        in_specs=(
            P(("dp", "et"), None),
            P(("dp", "et"), None),
            P(("dp", "et")),
            P(),
            P(None, None, "et"),
            P(None, None, "et"),
            P(None, "et", None),
        ),
        out_specs=(
            P(("dp", "et"), None),
            P(("dp", "et")),
            P(("dp", "et"), None),
            P(None, "dp", "et"),
            P(None, "dp", "et"),
            P(None, "et", "dp"),
        ),
        check_vma=False,
    )
```

time: 242 us -> 175 us (0.72)
  Pallas kernels: 206 us -> 162 us
  local copies, waits for them, and re-layouts: 30.5 us -> 4.93 us
    pallas_call x4, Pallas kernels: 148 us -> 112 us  [the longest x1 44.9 us: gather_rows(): pl.pallas_call(functools.partial(gather_kernel, cap), out_shape=(shape, s...]
    unnamed x15 -> x2, local copies, waits for them, and re-layouts: 29.8 us -> 1.4 us
    pallas_call x1, Pallas kernels: 58.1 us -> 50.3 us  [exchange(): pl.pallas_call(functools.partial(exchange_kernel, r), out_shape=jax.Shape...]
    another operation x0 -> x3, local copies, waits for them, and re-layouts: none -> 2.69 us
where the time goes in v2:
time: 175 us; the launch traced here: 174 us
  Pallas kernels  162 us (93%)
  local copies, waits for them, and re-layouts  4.93 us (3%)
  other arithmetic  4.34 us (2%)
  between operations  1.98 us (1%)
    pallas_call x1, Pallas kernels, exchange(): pl.pallas_call(functools.partial(exchange_kernel, r), out_shape=jax.Shape...  50.3 us
    pallas_call x1, Pallas kernels, gather_rows(): pl.pallas_call(functools.partial(gather_kernel, cap), out_shape=(shape, s...  44.9 us
    pallas_call x1, Pallas kernels, reduce_rows(): pl.pallas_call(functools.partial(reduce_kernel, cap), out_shape=(s((OWN,...  42.8 us
    pallas_call x1, Pallas kernels, second_matmuls(): pl.pallas_call(functools.partial(second_kernel, cap), out_shape=(s((n, DS...  14.1 us
    pallas_call x1, Pallas kernels, first_matmuls(): pl.pallas_call(functools.partial(first_kernel, cap), out_shape=(jax.Shape...  9.97 us

profile of v2, /device:TPU:1, one launch (start us, length us, event | category | flops | bytes accessed | tf_op | source)
XLA Modules:
  0.0 174.3 jit_solution(13665465545916011035)
XLA Ops:
  0.6 0.7 broadcast_compare_fusion
  1.3 0.7 broadcast_and_fusion
  2.0 0.7 broadcast_in_dim.35
  2.8 0.1 reshape.358
  2.9 0.1 fusion.8
  3.0 0.3 select_reduce_fusion.1
  3.3 0.1 broadcast_select_fusion
  3.4 0.6 reduce_max.9
  5.4 0.3 select_reduce_fusion
  5.8 166.5 %conditional.2 = (bf16[32,4096]{1,0:T(8,128)(2,1)S(1)}, f32[32,1]{1,0:T(8,128)S(1)}, bf16[32,4096]{1,0:T(8,128)(2,1)S(1)}, bf16[2,448,512]{2,1,0:T(8,128)(2,1)},...) conditional(s32[]{:T(128)} %clamp.8, (s32[8,2]{0,1:T(2,128)S(1)}, ...), branch_computations={%region_5.10_spmd.clone.clone, %region_10.11_spmd, %region_11.12_s... | conditional | flops 182 | bytes 1049552 | solution.py:716
  5.8 0.1 fusion.1
  5.9 0.6 fusion.2
  7.2 1.3 copy.32.cnt
  8.5 1.3 copy.31.rw_ref
  9.9 44.9 %gather_rows_8.3 = (bf16[4,4,8,16,512]{4,3,2,1,0:T(8,128)(2,1)}, bf16[4,4,8,16,512]{4,3,2,1,0:T(8,128)(2,1)}) custom-call(s32[32,16]{1,0:T(8,128)S(1)} %get-tuple-element.400.tab, bf16[32,4096]{1,0:T(8,128)(2,1)} %get-tuple-element.401.rows_ref, bf16[32,4096]{1,0:T(8,128)(2,1)} %get-tuple-element.402.oc_ref, f32[32,1]{1,0:T(8,128)} %copy.31.rw_ref), custom_call_target="tpu_custom_call" | custom-call | tf_op jit(solution)/shard_map/cond/branch_0_fun/gather_rows_8/pallas_call | solution.py:175
  54.8 10.0 %first_matmuls_8.3 = (bf16[2304,1344]{1,0:T(8,128)(2,1)}, bf16[2304,512]{1,0:T(8,128)(2,1)}, bf16[2304,512]{1,0:T(8,128)(2,1)}) custom-call(s32[8,2]{1,0:T(8,128)} %copy.32.cnt, s32[32,16]{1,0:T(8,128)S(1)} %get-tuple-element.400.tab, bf16[2048,512]{1,0:T(8,128)(2,1)} %bitcast.66, bf16[2048,512]{1,0:T(8,128)(2,1)} %bitcast.67, ...), custom_call_target="tpu_custom_call" | custom-call | tf_op jit(solution)/shard_map/cond/branch_0_fun/first_matmuls_8/pallas_call | solution.py:309
  64.8 50.3 %conditional.4 = (bf16[2304,1344]{1,0:T(8,128)(2,1)}) conditional(s32[]{:T(128)} %clamp.10, bf16[2304,1344]{1,0:T(8,128)(2,1)} %get-tuple-element.388, bf16[2304,1344]{1,0:T(8,128)(2,1)} %get-tuple-element.388, bf16[2304,1344]{1,0:T(8,128)(2,1)} %get-tuple-element.388), branch_computations={%region_7.7_spmd, %region_8.8_spmd, %region_9.9_spmd} | conditional | bytes 8 | solution.py:701
  64.8 50.3 %exchange_2_1536.1 = bf16[2304,1344]{1,0:T(8,128)(2,1)} custom-call(bf16[2304,1344]{1,0:T(8,128)(2,1)} %p), custom_call_target="tpu_custom_call" | custom-call | tf_op jit(solution)/shard_map/cond/branch_0_fun/cond/branch_0_fun/exchange_2_1536/pallas_call | solution.py:445
  115.1 0.0 copy-start
  115.1 14.1 %second_matmuls_8.3 = (bf16[2048,512]{1,0:T(8,128)(2,1)}, bf16[2048,512]{1,0:T(8,128)(2,1)}, bf16[2,448,512]{2,1,0:T(8,128)(2,1)}, bf16[2,448,512]{2,1,0:T(8,128)(2,1)}, bf16[2,448,512]{2,1,0:T(8,128)(2,1)}) custom-call(s32[8,2]{1,0:T(8,128)} %copy.32.cnt, s32[32,16]{1,0:T(8,128)S(1)} %get-tuple-element.400.tab, bf16[2304,1344]{1,0:T(8,128)(2,1)} %get-tuple-element.485.h, ...), custom_call_target="tpu_custom_call" | custom-call | tf_op jit(solution)/shard_map/cond/branch_0_fun/second_matmuls_8/pallas_call | solution.py:525
  129.2 0.0 copy-done
  129.3 42.8 %reduce_rows_8.3 = (bf16[32,4096]{1,0:T(8,128)(2,1)S(1)}, f32[32,1]{1,0:T(8,128)S(1)}, bf16[32,4096]{1,0:T(8,128)(2,1)S(1)}) custom-call(s32[32,16]{1,0:T(8,128)S(1)} %get-tuple-element.400.tab, bf16[4,4,8,16,512]{4,3,2,1,0:T(8,128)(2,1)} %bitcast.68, bf16[4,4,8,16,512]{4,3,2,1,0:T(8,128)(2,1)} %bitcast.69, f32[32,1]{1,0:T(8,128)} %copy.31.rw_ref, ...), custom_call_target="tpu_custom_call" | custom-call | tf_op jit(solution)/shard_map/cond/branch_0_fun/reduce_rows_8/pallas_call | solution.py:663
  172.3 0.6 reduce
  172.9 0.7 copy.56
  173.6 0.7 copy.57
  (6 shorter events, 0.0 us)
Async XLA Ops:
  115.1 14.2 %copy-start = (bf16[32,4096]{1,0:T(8,128)(2,1)S(1)}, bf16[32,4096]{1,0:T(8,128)(2,1)}, u32[]{:S(2)}) copy-start(bf16[32,4096]{1,0:T(8,128)(2,1)} %get-tuple-element.402.oc_ref) | copy-start | bytes 786436 | tf_op jit(solution)/shard_map/cond

commit v3 on v2

--- a/solution.py
+++ b/solution.py
@@ -17,7 +17,7 @@
 BR = 256
 T = 16
 TB = BR // T
-PLANS = ((8, (1536, 1792, 2304)), (10, (2816,)), (16, (ROWS + BR,)))
+PLANS = ((8, ((0, 3, 768), (3, 8, 768))), (10, ((0, 4, 1024), (4, 10, 1024))))
 VLIM = 60 * 1024 * 1024
 
 
@@ -677,45 +677,612 @@
     )(tab, o.reshape(4, 4, cap, T, DS), g.reshape(4, 4, cap, T, DS), rw, oc)
 
 
-def tile_tables(counts):
+def plan_kernel(plans, cnt, out):
+    i32 = lambda v: v.astype(jnp.int32)
+    f = lambda v: v.astype(F32)
     j = lax.broadcasted_iota(jnp.int32, (16, 16), 0)
     q = lax.broadcasted_iota(jnp.int32, (16, 16), 1)
     g, m = q // 2, q % 2
     s = origin(g, m, j)
-    c = jnp.repeat(counts, 2, axis=0)
-    n0, n1 = (c[:, 0] + T - 1) // T, (c[:, 1] + T - 1) // T
-    s1 = (c[:, 0] + 127) // 128 * 8
-    live = (s < n0) | ((s >= s1) & (s < s1 + n1))
-    one = live.astype(jnp.int32)
-    rank = jnp.sum(jnp.where(q[:, None, :] < q[:, :, None], one[:, None, :], 0), axis=2)
-    place = jnp.where(live, rank, -1)
-    order = jnp.sum(jnp.where(place[:, None, :] == q[:, :, None], q[:, None, :], 0), axis=2)
-    return jnp.concatenate([order, place], axis=0), jnp.max(jnp.sum(one, axis=1))
-
-
-def run(cap, levels, cid, rows, oc, rw, counts, tab, live, wg, wu, wd):
-    rmax = levels[-1]
-    xg, sg = gather_rows(cap, cid, tab, rows, oc, rw)
+    c0 = jnp.zeros((16, 16), jnp.int32)
+    c1 = jnp.zeros((16, 16), jnp.int32)
+    for k in range(GROUPS):
+        c0 = jnp.where(g == k, cnt[k, 0], c0)
+        c1 = jnp.where(g == k, cnt[k, 1], c1)
+    s1 = (c0 + 127) // 128 * 8
+    left0 = jnp.clip(c0 - T * s, 0, T)
+    left1 = jnp.where(s >= s1, jnp.clip(c1 - T * (s - s1), 0, T), 0)
+    live = left0 + left1 > 0
+    one = f(i32(live))
+    mm = lambda a, b, dims: lax.dot_general(a, b, (dims, ((), ())), preferred_element_type=F32,
+                                            precision=lax.Precision.HIGHEST)
+    rank = mm(one, f(i32(j < q)), ((1,), (0,)))
+    place = jnp.where(live, i32(rank), -1)
+    orders = jnp.zeros((16, 16), jnp.int32)
+    rows0 = jnp.zeros((16, 16), jnp.int32)
+    rows1 = jnp.zeros((16, 16), jnp.int32)
+    for k in range(16):
+        hit = place == k
+        pick = lambda v: jnp.sum(f(jnp.where(hit, v, 0)), axis=1, keepdims=True)
+        orders = jnp.where(q == k, i32(pick(q)), orders)
+        rows0 = jnp.where(q == k, i32(pick(left0)), rows0)
+        rows1 = jnp.where(q == k, i32(pick(left1)), rows1)
+    out[...] = jnp.zeros_like(out)
+    out[0:16, 0:16] = orders
+    out[16:32, 0:16] = place
+    nrow = mm(jnp.ones((8, 16), F32), one, ((1,), (1,)))[0:1, :]
+    ok = []
+    base = 32
+    for cap, chunks in plans:
+        fits = jnp.max(nrow) <= cap
+        for lo, hi, r in chunks:
+            nt = r // T
+            n = jnp.clip(nrow - lo, 0.0, float(hi - lo))
+            n8 = jnp.broadcast_to(n, (8, 16))
+            off = mm(n8, f(i32(j < q)), ((1,), (0,)))[0:1, :]
+            t = lax.broadcasted_iota(jnp.int32, (nt, 16), 0)
+            qq = lax.broadcasted_iota(jnp.int32, (nt, 16), 1)
+            offb, nb = jnp.broadcast_to(off, (nt, 16)), jnp.broadcast_to(n, (nt, 16))
+            hot = f(i32((f(t) >= offb) & (f(t) < offb + nb)))
+            at = jnp.sum(hot * (f(t) - offb), axis=1, keepdims=True)
+            dev = jnp.sum(hot * f(qq), axis=1, keepdims=True)
+            used = jnp.sum(hot, axis=1, keepdims=True)
+            col = f(i32(f(qq) == at + float(lo)))
+            sel = lambda v: jnp.sum(col * mm(hot, f(v), ((1,), (0,))), axis=1, keepdims=True) * used
+            out[base:base + nt, 0:1] = i32(dev * float(hi - lo) + at)
+            out[base:base + nt, 1:2] = i32(sel(rows0))
+            out[base:base + nt, 2:3] = i32(sel(rows1))
+            ncol = jnp.clip(jnp.sum(one, axis=1, keepdims=True) - lo, 0.0, float(hi - lo))
+            ocol = mm(f(i32(q < j)), jnp.broadcast_to(ncol, (16, 8)), ((1,), (0,)))[:, 0:1]
+            back = jnp.clip(i32(ocol) + q - lo, 0, nt - 1)
+            out[base + nt:base + nt + 16, 0:16] = back + jnp.where(rows1 > 0, nt, 0)
+            base += nt + 16
+            fits = jnp.logical_and(fits, jnp.sum(n) <= nt)
+        ok.append(fits)
+    level = jnp.int32(len(plans))
+    for i in range(len(plans) - 1, -1, -1):
+        level = jnp.where(ok[i], i, level)
+    lane = lax.broadcasted_iota(jnp.int32, (8, 16), 1)
+    out[base:base + 8, 0:16] = jnp.where(lane == 0, level, 0)
+
+
+def table_base(plans, index):
+    base = 32
+    for cap, chunks in plans[:index]:
+        for lo, hi, r in chunks:
+            base += r // T + 16
+    return base
+
+
+def plan_table(plans, counts):
+    rows = table_base(plans, len(plans)) + 8
+    return pl.pallas_call(
+        functools.partial(plan_kernel, plans),
+        out_shape=jax.ShapeDtypeStruct((rows, 16), jnp.int32),
+        in_specs=[pl.BlockSpec(memory_space=pltpu.SMEM)],
+        out_specs=pl.BlockSpec(memory_space=pltpu.VMEM),
+        name="tile_plan",
+    )(counts)
+
+
+def layer_kernel(cap, chunks, base, tab, rows_ref, oc_ref, rw_ref, wg, wu, wd,
+                 out_o, out_w, out_g, dg, du, dd_o, sc, rb0, rb1, stage, wcat, xcat, scat, hall,
+                 ov, gv, fin, ex, rec, *rest):
+    d, j = lax.axis_index("dp"), lax.axis_index("et")
+    me = (d, j)
+    y, x = j // 4, j % 4
+    z, c = d // 2, d % 2
+    nch = len(chunks)
+    names = ("xg", "sg", "part", "prt", "q", "zl1", "zr1", "zs1", "zs2", "zl2", "zr2", "tot",
+             "ob", "gb", "l1", "r1", "s1", "s2", "l2", "r2", "acc", "bl1", "br1", "bs1", "bs2", "bl2", "br2")
+    buf = [dict(zip(names, rest[i * len(names):(i + 1) * len(names)])) for i in range(nch)]
+    (psend, precv, wsem, rsend, rrecv, zps, zpr, zbs, zbr, zgs, zgr,
+     asend, arecv, bsend, brecv, qsend, qrecv) = rest[nch * len(names):]
+    up, down = {"dp": (z + 1) % 4 * 2 + c}, {"dp": (z + 3) % 4 * 2 + c}
+    mate = {"dp": z * 2 + 1 - c}
+    owners = [((d + k) % 8, spot(d, 2 * j + hh)) for k in range(8) for hh in range(2)]
+    senders = [((d + 8 - k) % 8, origin((d + 8 - k) % 8, m, j) // 2) for k in range(8) for m in range(2)]
+    greet([plane("x", x + 1, j), plane("x", x + 3, j), plane("y", y + 1, j), plane("y", y + 3, j),
+           up, down, mate], owners + senders)
+    finish = []
+    rb = (rb0, rb1)
+    offs = []
+    b = base
+    for lo, hi, r in chunks:
+        offs.append(b)
+        b += r // T + 16
+    first_row = [sum(r for _, _, r in chunks[:i]) for i in range(nch)]
+
+    def remote(src, dst, ssem, rsem, dev):
+        cp = rcopy(src, dst, ssem, rsem, dev)
+        cp.start()
+        finish.append(cp.wait_send)
+        return cp
+
+    mm = j // 8
+    cols = pl.ds(pl.multiple_of(d * DS, DS), DS)
+    wcp = []
+    for a, src in enumerate((rows_ref, sc)):
+        if a == 1:
+            eye = lax.broadcasted_iota(jnp.int32, (OWN, OWN), 0) == lax.broadcasted_iota(jnp.int32, (OWN, OWN), 1)
+            rw = jnp.sum(jnp.where(eye, jnp.broadcast_to(rw_ref[...], (OWN, OWN)), 0.0), axis=1, keepdims=True)
+            for k in range(8):
+                cs = slice(k * DS, (k + 1) * DS)
+                sc[:, cs] = (rw * oc_ref[:, cs].astype(F32)).astype(BF)
+        for k in range(8):
+            dd = (d + k) % 8
+            cs = pl.ds(pl.multiple_of(dd * DS, DS), DS)
+            for hh in range(2):
+                jj = spot(d, 2 * j + hh)
+                finish.append(deliver(me, src.at[pl.ds(T * hh, T), cs], rb[a].at[2 * d + mm],
+                                      psend.at[a, k, hh], precv.at[a, k, mm], dd, jj))
+    for e in range(2):
+        for i, w in enumerate((wg, wu, wd)):
+            cp = pltpu.make_async_copy(w.at[e, :, cols],
+                                       wcat.at[pl.ds(i * HID, HID), pl.ds(e * DS, DS)], wsem.at[e, i])
+            cp.start()
+            wcp.append(cp)
+
+    def arrive(a):
+        for k in range(8):
+            for m in range(2):
+                ref = rb[a].at[2 * ((d + 8 - k) % 8) + m]
+                pltpu.make_async_copy(ref, ref, precv.at[a, k, m]).wait()
+        for i in range(cap):
+            stage[a, i] = rb[a][tab[j, i]]
+
+    def gather(ch):
+        lo, hi, r = chunks[ch]
+        nt = hi - lo
+        h0 = nt // 2
+        ax = (("x", "y", x, y), ("y", "x", y, x))
+        outs = (buf[ch]["xg"], buf[ch]["sg"])
+
+        def blk(a, pp, qq, half=None):
+            yy, xx = (qq % 4, pp % 4) if a == 0 else (pp % 4, qq % 4)
+            off, n = (0, nt) if half is None else ((0, h0) if half == 0 else (h0, nt - h0))
+            return outs[a].at[pl.ds((4 * yy + xx) * nt + off, n)]
+
+        sent = [dict(), dict()]
+
+        def send(a, i, ref, axis, pos, own=None):
+            sent[a][i] = remote(ref if own is None else own, ref, rsend.at[ch, a, i], rrecv.at[ch, a, i],
+                                plane(axis, pos, j))
+
+        def seconds(a, u, own=None):
+            first, second, p, q = ax[a]
+            i = 4 + 4 * (u % 4)
+            send(a, i, blk(a, p + u, q), second, q + 1, own)
+            send(a, i + 1, blk(a, p + u, q), second, q + 3, own)
+
+        def forward(a, u):
+            first, second, p, q = ax[a]
+            i = 4 + 4 * (u % 4)
+            sent[a][i].wait_recv()
+            send(a, i + 2, blk(a, p + u, q + 3, 0), second, q + 1)
+            sent[a][i + 1].wait_recv()
+            send(a, i + 3, blk(a, p + u, q + 1, 1), second, q + 3)
+
+        for a in range(2):
+            first, second, p, q = ax[a]
+            if ch == 0:
+                arrive(a)
+            own = stage.at[a, pl.ds(lo, nt)]
+            send(a, 0, blk(a, p, q), first, p + 1, own)
+            send(a, 1, blk(a, p, q), first, p + 3, own)
+            seconds(a, 0, own)
+            outs[a][pl.ds(j * nt, nt)] = stage[a, lo:hi]
+        yield
+        for a in range(2):
+            first, second, p, q = ax[a]
+            sent[a][0].wait_recv()
+            send(a, 2, blk(a, p + 3, q, 0), first, p + 1)
+            seconds(a, 3)
+            sent[a][1].wait_recv()
+            send(a, 3, blk(a, p + 1, q, 1), first, p + 3)
+            seconds(a, 1)
+            yield
+        for a in range(2):
+            forward(a, 0)
+            yield
+        for a in range(2):
+            sent[a][2].wait_recv()
+            sent[a][3].wait_recv()
+            seconds(a, 2)
+        yield
+        for u in (3, 1, 2):
+            for a in range(2):
+                forward(a, u)
+            yield
+        for a in range(2):
+            for u in range(4):
+                sent[a][6 + 4 * u].wait_recv()
+                sent[a][7 + 4 * u].wait_recv()
+
+    def first(ch):
+        lo, hi, r = chunks[ch]
+        xg, sg, part = buf[ch]["xg"], buf[ch]["sg"], buf[ch]["part"]
+        iota = lax.broadcasted_iota(jnp.int32, (T, DS), 0)
+        r0 = first_row[ch]
+
+        def pack(t, _):
+            src = tab[offs[ch] + t, 0]
+            xt, st = xg[src].astype(F32), sg[src].astype(F32)
+            dst = tile(r0 // T + t)
+            for e in range(2):
+                keep = iota < tab[offs[ch] + t, 1 + e]
+                cs = slice(e * DS, (e + 1) * DS)
+                xcat[dst, cs] = jnp.where(keep, xt, 0.0).astype(BF)
+                scat[dst, cs] = jnp.where(keep, st, 0.0).astype(BF)
+            return 0
+
+        lax.fori_loop(0, r // T, pack, 0)
+        if ch == 0:
+            for cp in wcp:
+                cp.wait()
+
+        def mul(i, _):
+            src = pl.ds(pl.multiple_of(r0 + i * BR, BR), BR)
+            dst = rows_of(i)
+            part[dst, 0:H2] = lax.dot_general(
+                xcat[src, :], wcat[0:H2, :], TRANS_R, preferred_element_type=F32).astype(BF)
+            part[dst, H2:H3] = lax.dot_general(
+                scat[src, :], wcat[H2:H3, :], TRANS_R, preferred_element_type=F32).astype(BF)
+            return 0
+
+        lax.fori_loop(0, r // BR, mul, 0)
+
+    def exchange_chunk(ch):
+        lo, hi, r = chunks[ch]
+        bf = buf[ch]
+        part, prt, q, tot = bf["part"], bf["prt"], bf["q"], bf["tot"]
+        r8, r16 = r // 8, r // 16
+        r0 = first_row[ch]
+        fst, snd = pl.ds(0, r16), pl.ds(r16, r16)
+
+        def rows(zz, cc, off=0, n=None):
+            return pl.ds(pl.multiple_of((zz % 4 * 2 + cc) * r8 + off, 16), r8 if n is None else n)
+
+        def hrows(zz, cc, off=0, n=None):
+            return hall.at[pl.ds(pl.multiple_of(r0 + (zz % 4 * 2 + cc) * r8 + off, 16), r8 if n is None else n)]
+
+        pair = {}
+        for i in (2, 1, 3, 0):
+            pair[i] = remote(part.at[rows(z + i, 1 - c)], prt.at[i], zps.at[ch, i], zpr.at[ch, i], mate)
+        yield
+
+        def bsum(i):
+            pair[i].wait_recv()
+            start = (z + i) % 4 * 2 + c
+
+            def one(k, _):
+                src = pl.ds(pl.multiple_of(start * r8 + k * T, T), T)
+                q[i, tile(k), :] = (part[src, :].astype(F32) + prt[i, tile(k), :].astype(F32)).astype(BF)
+                return 0
+
+            lax.fori_loop(0, r8 // T, one, 0)
+
+        def add_rows(dst, src, i, off):
+            def one(k, _):
+                dst[tile(k), :] = (src[tile(k), :].astype(F32) + q[i, tile(off + k), :].astype(F32)).astype(BF)
+                return 0
+
+            lax.fori_loop(0, r16 // T, one, 0)
+
+        def push(i, src, dst, dev):
+            return remote(src, dst, zbs.at[ch, i], zbr.at[ch, i], dev)
+
+        bsum(2)
+        a_l = push(0, q.at[2, fst], bf["zl1"], up)
+        a_r = push(1, q.at[2, snd], bf["zr1"], down)
+        bsum(1)
+        b_l2 = push(2, q.at[1, snd], bf["zl2"].at[snd], up)
+        bsum(3)
+        b_r1 = push(3, q.at[3, fst], bf["zr2"].at[fst], down)
+        yield
+        a_l.wait_recv()
+        add_rows(bf["zs1"], bf["zl1"], 1, 0)
+        b_l1 = push(4, bf["zs1"], bf["zl2"].at[fst], up)
+        a_r.wait_recv()
+        add_rows(bf["zs2"], bf["zr1"], 3, r16 // T)
+        b_r2 = push(5, bf["zs2"], bf["zr2"].at[snd], down)
+        yield
+        pair[0].wait_recv()
+        for cp in (b_l2, b_r1, b_l1, b_r2):
+            cp.wait_recv()
+        mine = (z * 2 + c) * r8
+
+        def final(k, _):
+            t = tile(k)
+            src = pl.ds(pl.multiple_of(mine + k * T, T), T)
+            dst = pl.ds(pl.multiple_of(r0 + mine + k * T, T), T)
+            tot[...] = (part[src, :].astype(F32) + prt[0, t, :].astype(F32)
+                        + bf["zl2"][t, :].astype(F32) + bf["zr2"][t, :].astype(F32))
+            gate, lin, grad = tot[:, 0:HID], tot[:, HID:H2], tot[:, H2:H3]
+            s = 1.0 / (1.0 + jnp.exp(-gate))
+            act = gate * s
+            hall[dst, 0:HID] = (grad * lin * s * (1.0 + gate * (1.0 - s))).astype(BF)
+            hall[dst, HID:H2] = (grad * act).astype(BF)
+            hall[dst, H2:H3] = (act * lin).astype(BF)
+            return 0
+
+        lax.fori_loop(0, r8 // T, final, 0)
+        gps = {}
+
+        def spread(i, ref, dev):
+            gps[i] = remote(ref, ref, zgs.at[ch, i], zgr.at[ch, i], dev)
+
+        spread(0, hrows(z, c), up)
+        spread(1, hrows(z, c), down)
+        spread(2, hrows(z, c), mate)
+        yield
+        gps[0].wait_recv()
+        spread(3, hrows(z + 3, c, 0, r16), up)
+        spread(4, hrows(z + 3, c), mate)
+        gps[1].wait_recv()
+        spread(5, hrows(z + 1, c, r16, r16), down)
+        spread(6, hrows(z + 1, c), mate)
+        yield
+        gps[3].wait_recv()
+        spread(7, hrows(z + 2, c, 0, r16), mate)
+        gps[5].wait_recv()
+        spread(8, hrows(z + 2, c, r16, r16), mate)
+        yield
+        for i in (2, 4, 6, 7, 8):
+            gps[i].wait_recv()
+
+    def second(ch):
+        lo, hi, r = chunks[ch]
+        nt = hi - lo
+        r0 = first_row[ch]
+        ob, gb = buf[ch]["ob"], buf[ch]["gb"]
+
+        def mul(i, _):
+            src = pl.ds(pl.multiple_of(r0 + i * BR, BR), BR)
+            for e in range(2):
+                dst = pl.ds(e * (r // T) + i * TB, TB)
+                cs = slice(e * DS, (e + 1) * DS)
+                to = jnp.dot(hall[src, H2:H3], wcat[H2:H3, cs], preferred_element_type=F32).astype(BF)
+                tg = jnp.dot(hall[src, 0:H2], wcat[0:H2, cs], preferred_element_type=F32).astype(BF)
+                ov[dst] = to.reshape(TB, T, DS)
+                gv[dst] = tg.reshape(TB, T, DS)
+            return 0
+
+        lax.fori_loop(0, r // BR, mul, 0)
+
+        def unpack(jj, _):
+            for i in range(nt):
+                src = tab[offs[ch] + r // T + jj, lo + i]
+                ob[jj, i] = ov[src]
+                gb[jj, i] = gv[src]
+            return 0
+
+        lax.fori_loop(0, 16, unpack, 0)
+
+    def reduce_chunk(ch):
+        lo_t, hi_t, r = chunks[ch]
+        nt = hi_t - lo_t
+        h0 = nt // 2
+        bf = buf[ch]
+        lo, hi = pl.ds(0, h0), pl.ds(h0, nt - h0)
+        srcs = (bf["ob"], bf["gb"])
+        ax = (("y", "x", y, x), ("x", "y", x, y))
+        order = (2, 1, 3, 0)
+
+        def blk(a, pp, qq, g):
+            yy, xx = (pp % 4, qq % 4) if a == 0 else (qq % 4, pp % 4)
+            return srcs[a].at[4 * yy + xx, g]
+
+        def push(sems, key, src, dst, axis, pos):
+            return remote(src, dst, sems[0].at[(ch,) + key], sems[1].at[(ch,) + key], plane(axis, pos, j))
+
+        def add2(n, dst, b, cc):
+            for g in range(n):
+                dst[g] = (b[g].astype(F32) + cc[g].astype(F32)).astype(BF)
+
+        A, B = (asend, arecv), (bsend, brecv)
+        av, bv = [dict(), dict()], [dict(), dict()]
+        l1, r1, s1, s2, l2, r2, acc = (bf[k] for k in ("l1", "r1", "s1", "s2", "l2", "r2", "acc"))
+        bl1, br1, bs1, bs2, bl2, br2 = (bf[k] for k in ("bl1", "br1", "bs1", "bs2", "bl2", "br2"))
+        for u in order:
+            for a in range(2):
+                fx, sx, p, q = ax[a]
+                av[a][u, 0] = push(A, (a, u, 0), blk(a, p + 2, q + u, lo), l1.at[a, u], fx, p + 1)
+                av[a][u, 1] = push(A, (a, u, 1), blk(a, p + 2, q + u, hi), r1.at[a, u], fx, p + 3)
+                av[a][u, 2] = push(A, (a, u, 2), blk(a, p + 1, q + u, hi), l2.at[a, u, hi], fx, p + 1)
+                av[a][u, 3] = push(A, (a, u, 3), blk(a, p + 3, q + u, lo), r2.at[a, u, lo], fx, p + 3)
+        yield
+        for u in order:
+            for a in range(2):
+                fx, sx, p, q = ax[a]
+                av[a][u, 0].wait_recv()
+                add2(h0, s1.at[a, u], l1.at[a, u], blk(a, p + 1, q + u, lo))
+                av[a][u, 4] = push(A, (a, u, 4), s1.at[a, u], l2.at[a, u, lo], fx, p + 1)
+                av[a][u, 1].wait_recv()
+                add2(nt - h0, s2.at[a, u], r1.at[a, u], blk(a, p + 3, q + u, hi))
+                av[a][u, 5] = push(A, (a, u, 5), s2.at[a, u], r2.at[a, u, hi], fx, p + 3)
+            if u in (1, 0):
+                yield
+        for u in order:
+            for a in range(2):
+                fx, sx, p, q = ax[a]
+                for i in (2, 3, 4, 5):
+                    av[a][u, i].wait_recv()
+                mine = blk(a, p, q + u, pl.ds(0, nt))
+                for g in range(nt):
+                    acc[a, u, g] = (mine[g].astype(F32) + l2[a, u, g].astype(F32)
+                                    + r2[a, u, g].astype(F32)).astype(BF)
+                if u == 2:
+                    bv[a][0] = push(B, (a, 0), acc.at[a, 2, lo], bl1.at[a], sx, q + 1)
+                    bv[a][1] = push(B, (a, 1), acc.at[a, 2, hi], br1.at[a], sx, q + 3)
+                elif u == 1:
+                    bv[a][2] = push(B, (a, 2), acc.at[a, 1, hi], bl2.at[a, hi], sx, q + 1)
+                elif u == 3:
+                    bv[a][3] = push(B, (a, 3), acc.at[a, 3, lo], br2.at[a, lo], sx, q + 3)
+            if u in (1, 0):
+                yield
+        for a in range(2):
+            fx, sx, p, q = ax[a]
+            bv[a][0].wait_recv()
+            add2(h0, bs1.at[a], bl1.at[a], acc.at[a, 1, lo])
+            bv[a][4] = push(B, (a, 4), bs1.at[a], bl2.at[a, lo], sx, q + 1)
+            bv[a][1].wait_recv()
+            add2(nt - h0, bs2.at[a], br1.at[a], acc.at[a, 3, hi])
+            bv[a][5] = push(B, (a, 5), bs2.at[a], br2.at[a, hi], sx, q + 3)
+        yield
+        for a in range(2):
+            for i in (2, 3, 4, 5):
+                bv[a][i].wait_recv()
+            for g in range(nt):
+                fin[a, lo_t + g] = (acc[a, 0, g].astype(F32) + bl2[a, g].astype(F32)
+                                    + br2[a, g].astype(F32)).astype(BF)
+
+    def weight_grads():
+        n = 256
+
+        def one(i, _):
+            cs = pl.ds(pl.multiple_of(i * n, n), n)
+            e, os = i // (DS // n), pl.ds(pl.multiple_of(i % (DS // n) * n, n), n)
+            both = lax.dot_general(hall[:, 0:H2], xcat[:, cs], TRANS_L, preferred_element_type=F32)
+            dg[e, :, os] = both[0:HID].astype(BF)
+            du[e, :, os] = both[HID:H2].astype(BF)
+            dd_o[e, :, os] = lax.dot_general(hall[:, H2:H3], scat[:, cs], TRANS_L,
+                                             preferred_element_type=F32).astype(BF)
+            return 0
+
+        lax.fori_loop(0, 2 * DS // n, one, 0)
+
+    def drain(gen):
+        for _ in gen:
+            pass
+
+    def step(gen, n=1):
+        for _ in range(n):
+            if next(gen, 0) == 0:
+                return False
+        return True
+
+    drain(gather(0))
+    first(0)
+    if nch == 2:
+        za, gb_ = exchange_chunk(0), gather(1)
+        step(za)
+        more = True
+        while step(za):
+            more = more and step(gb_, 2)
+        drain(gb_)
+        first(1)
+        zb = exchange_chunk(1)
+        step(zb)
+        second(0)
+        ra = reduce_chunk(0)
+        step(ra)
+        while step(zb):
+            step(ra)
+        drain(ra)
+        second(1)
+        rl = reduce_chunk(1)
+    else:
+        drain(exchange_chunk(0))
+        second(0)
+        rl = reduce_chunk(0)
+    step(rl)
+    weight_grads()
+    drain(rl)
+
+    for a in range(2):
+        for k in range(8):
+            g = (d + k) % 8
+            for m in range(2):
+                s = origin(g, m, j)
+                at = tab[16 + j, 2 * g + m]
+                got = fin[a, jnp.maximum(at, 0)].astype(F32)
+                ex[a, k, m] = jnp.where(at >= 0, got, 0.0).astype(BF)
+                finish.append(deliver(me, ex.at[a, k, m], rec.at[a, d, s % 2],
+                                      qsend.at[a, k, m], qrecv.at[a, k, s % 2], g, s // 2))
+    total = jnp.zeros((OWN, 1), F32)
+    for a in range(2):
+        for k in range(8):
+            for hh in range(2):
+                ref = rec.at[a, (d + 8 - k) % 8, hh]
+                pltpu.make_async_copy(ref, ref, qrecv.at[a, k, hh]).wait()
+        for k in range(8):
+            cs = slice(k * DS, (k + 1) * DS)
+            if a == 0:
+                comb = rec[0, k].astype(F32).reshape(OWN, DS)
+                out_o[:, cs] = (rw * comb).astype(BF)
+                total = total + jnp.sum(oc_ref[:, cs].astype(F32) * comb, axis=1, keepdims=True)
+            else:
+                out_g[:, cs] = rec[1, k].reshape(OWN, DS)
+    out_w[...] = jnp.sum(jnp.where(eye, jnp.broadcast_to(total, (OWN, OWN)), 0.0), axis=0, keepdims=True)
+    for f in finish:
+        f()
+
+
+def layer(plans, index, cid, tab, rows, oc, rw, wg, wu, wd):
+    cap, chunks = plans[index]
+    vm = pl.BlockSpec(memory_space=pltpu.VMEM)
+    any_ = pl.BlockSpec(memory_space=pl.ANY)
+    s = jax.ShapeDtypeStruct
+    v = lambda *sh: pltpu.VMEM(sh, BF)
+    tl = lambda *sh: pltpu.VMEM(sh + (T, DS), BF)
+    dma = lambda *n: pltpu.SemaphoreType.DMA(n)
+    total = sum(r for _, _, r in chunks)
+    rbig = max(r for _, _, r in chunks)
+    nch = len(chunks)
+    scratch = [v(OWN, DM), tl(16), tl(16), tl(2, cap), v(H3, 2 * DS), v(total, 2 * DS), v(total, 2 * DS),
+               v(total, H3), tl(2 * rbig // T), tl(2 * rbig // T), tl(2, cap), tl(2, 8, 2), tl(2, 8, 2)]
+    for lo, hi, r in chunks:
+        nt = hi - lo
+        h0, h1 = nt // 2, nt - nt // 2
+        r8, r16 = r // 8, r // 16
+        scratch += [tl(16 * nt), tl(16 * nt), v(r, H3), v(4, r8, H3), v(4, r8, H3),
+                    v(r16, H3), v(r16, H3), v(r16, H3), v(r16, H3), v(r8, H3), v(r8, H3),
+                    pltpu.VMEM((T, H3), F32), tl(16, nt), tl(16, nt),
+                    tl(2, 4, h0), tl(2, 4, h1), tl(2, 4, h0), tl(2, 4, h1),
+                    tl(2, 4, nt), tl(2, 4, nt), tl(2, 4, nt),
+                    tl(2, h0), tl(2, h1), tl(2, h0), tl(2, h1), tl(2, nt), tl(2, nt)]
+    scratch += [dma(2, 8, 2), dma(2, 8, 2), dma(2, 3), dma(nch, 2, 20), dma(nch, 2, 20),
+                dma(nch, 4), dma(nch, 4), dma(nch, 6), dma(nch, 6), dma(nch, 9), dma(nch, 9),
+                dma(nch, 2, 4, 6), dma(nch, 2, 4, 6), dma(nch, 2, 6), dma(nch, 2, 6),
+                dma(2, 8, 2), dma(2, 8, 2)]
+    w = s((2, HID, DS), BF)
+    return pl.pallas_call(
+        functools.partial(layer_kernel, cap, chunks, table_base(plans, index)),
+        out_shape=(s((OWN, DM), BF), s((1, OWN), F32), s((OWN, DM), BF), w, w, w),
+        in_specs=[pl.BlockSpec(memory_space=pltpu.SMEM), vm, vm, vm, any_, any_, any_],
+        out_specs=(vm,) * 6,
+        scratch_shapes=scratch,
+        compiler_params=pltpu.CompilerParams(
+            collective_id=cid, has_side_effects=True, vmem_limit_bytes=VLIM),
+        name="layer_%d_%d" % (cap, total),
+    )(tab, rows, oc, rw, wg, wu, wd)
+
+
+def run(rows, oc, rw, counts, tab, wg, wu, wd):
+    cap, rmax = 16, ROWS + BR
+    rw = rw.reshape(OWN, 1)
+    xg, sg = gather_rows(cap, 0, tab, rows, oc, rw)
     part, xc, sc = first_matmuls(cap, rmax, counts, tab, xg, sg, wg, wu, wd)
-    level = sum((live > r).astype(jnp.int32) for r in levels[:-1])
-    h = lax.switch(level, [functools.partial(exchange, r, rmax, cid + 2 + i)
-                           for i, r in enumerate(levels)], part)
+    h = exchange(rmax, rmax, 1, part)
     o, gr, dg, du, dd = second_matmuls(cap, rmax, counts, tab, h, xc, sc, wg, wu, wd)
-    layer_out, grad_weight, grad_rows = reduce_rows(cap, cid + 1, tab, o, gr, rw, oc)
-    return layer_out, grad_weight, grad_rows, dg, du, dd
+    layer_out, grad_weight, grad_rows = reduce_rows(cap, 2, tab, o, gr, rw, oc)
+    return layer_out, grad_weight.reshape(1, OWN), grad_rows, dg, du, dd
 
 
 def per_device(routed_rows, out_cotangent, route_weight, expert_counts, w_gate, w_up, w_down):
-    rw = route_weight[:, None]
+    rw = route_weight.reshape(1, OWN)
     wg, wu = jnp.swapaxes(w_gate, 1, 2), jnp.swapaxes(w_up, 1, 2)
-    tab, most = tile_tables(expert_counts)
-    tiles = jnp.sum((expert_counts + T - 1) // T, axis=0)
-    live = jnp.sum((tiles + TB - 1) // TB) * BR
-    pick = sum((most > cap).astype(jnp.int32) for cap, _ in PLANS[:-1])
-    branches = [functools.partial(run, cap, levels, 8 * i) for i, (cap, levels) in enumerate(PLANS)]
+    tab = plan_table(PLANS, expert_counts)
+    pick = tab[table_base(PLANS, len(PLANS)), 0]
+
+    def fast(i, rows, oc, rw, counts, tab, wg, wu, wd):
+        return layer(PLANS, i, 3 + i, tab, rows, oc, rw, wg, wu, wd)
+
+    branches = [functools.partial(fast, i) for i in range(len(PLANS))] + [run]
     layer_out, grad_weight, grad_rows, dg, du, dd = lax.switch(
-        pick, branches, routed_rows, out_cotangent, rw, expert_counts, tab, live, wg, wu, w_down)
-    return (layer_out, grad_weight[:, 0], grad_rows,
+        pick, branches, routed_rows, out_cotangent, rw, expert_counts, tab, wg, wu, w_down)
+    return (layer_out, grad_weight.reshape(OWN), grad_rows,
             jnp.swapaxes(dg, 1, 2), jnp.swapaxes(du, 1, 2), dd)
 
 

time: 175 us -> 155 us (0.89)
  Pallas kernels: 162 us -> 145 us
  other arithmetic: 4.34 us -> 0 us
  local copies, waits for them, and re-layouts: 4.93 us -> 7.51 us
    pallas_call x5 -> x2, Pallas kernels: 162 us -> 145 us  [the longest x1 143 us: layer(): pl.pallas_call(functools.partial(layer_kernel, cap, chunks, table_base(pl...]
    unnamed x2 -> x7, local copies, waits for them, and re-layouts: 1.4 us -> 7 us
    another operation x3 -> x0, local copies, waits for them, and re-layouts: 2.69 us -> none
where the time goes in v3:
time: 155 us; the launch traced here: 154 us
  Pallas kernels  145 us (94%)
  local copies, waits for them, and re-layouts  7.51 us (5%)
    pallas_call x1, Pallas kernels, layer(): pl.pallas_call(functools.partial(layer_kernel, cap, chunks, table_base(pl...  143 us
    unnamed x7, local copies, waits for them, and re-layouts  7 us

profile of v3, /device:TPU:1, one launch (start us, length us, event | category | flops | bytes accessed | tf_op | source)
XLA Modules:
  0.0 154.0 jit_solution(5737798079962176148)
XLA Ops:
  0.6 1.3 copy.19.cnt
  2.0 2.0 %tile_plan.1 = s32[328,16]{1,0:T(8,128)S(1)} custom-call(s32[8,2]{1,0:T(8,128)} %copy.19.cnt), custom_call_target="tpu_custom_call" | custom-call | tf_op jit(solution)/shard_map/tile_plan/pallas_call | solution.py:759
  4.0 0.5 slice.4
  5.1 143.2 %conditional.1 = (bf16[32,4096]{1,0:T(8,128)(2,1)S(1)}, bf16[32,4096]{1,0:T(8,128)(2,1)}, bf16[2,448,512]{2,1,0:T(8,128)(2,1)S(1)}, bf16[2,448,512]{2,1,0:T(8,12...) conditional(s32[]{:T(128)} %bitcast.9, (f32[32]{0:T(128)}, ...), branch_computations={%region_0.0_spmd, %region_1.0_spmd, %region_2.0_spmd} | conditional | bytes 1049296 | solution.py:1283
  5.1 143.0 %layer_8_1536.1 = (bf16[32,4096]{1,0:T(8,128)(2,1)S(1)}, f32[1,32]{1,0:T(1,128)S(1)}, bf16[32,4096]{1,0:T(8,128)(2,1)}, bf16[2,448,512]{2,1,0:T(8,128)(2,1)S(1)}...) custom-call(s32[328,16]{1,0:T(8,128)S(1)} %get-tuple-element.59.tab, ...), custom_call_target="tpu_custom_call" | custom-call | tf_op jit(solution)/shard_map/cond/branch_0_fun/layer_8_1536/pallas_call | solution.py:1250
  148.3 0.7 copy.45
  149.0 0.5 copy.46
  149.6 1.7 %copy.47 = bf16[32,4096]{1,0:T(8,128)(2,1)} copy(bf16[32,4096]{1,0:T(8,128)(2,1)} %get-tuple-element.166) | data formatting | bytes 524288
  151.2 0.9 copy.48
  152.2 0.9 copy.49
  153.1 0.9 copy.50

commit v4 on v3

--- a/solution.py
+++ b/solution.py
@@ -17,7 +17,7 @@
 BR = 256
 T = 16
 TB = BR // T
-PLANS = ((8, ((0, 3, 768), (3, 8, 768))), (10, ((0, 4, 1024), (4, 10, 1024))))
+PLANS = ((8, ((0, 3, 768), (3, 8, 768))), (10, ((0, 4, 1024), (4, 10, 768))))
 VLIM = 60 * 1024 * 1024
 
 
@@ -200,8 +200,8 @@
     for e in range(2):
         row = []
         for g in range(GROUPS):
-            c = cnt[g, e]
-            first = 0 if e == 0 else (cnt[g, 0] + 127) // 128 * 8
+            c = cnt[e, g]
+            first = 0 if e == 0 else (cnt[0, g] + 127) // 128 * 8
             n = (c + T - 1) // T
             row.append((c, first, n, t))
             t = t + n
@@ -245,7 +245,7 @@
 
     def source(g, s):
         jj = spot(g, s)
-        return tile(jj * cap + tab[16 + jj, 2 * g + s // 16])
+        return tile(jj * cap + tab[jj, 16 + 2 * g + s // 16])
 
     for e in range(2):
         for g in range(GROUPS):
@@ -508,7 +508,7 @@
             def move(k, _, g=g, first=first, t0=t0):
                 s = first + k
                 jj = spot(g, s)
-                dst = tile(jj * cap + tab[16 + jj, 2 * g + s // 16])
+                dst = tile(jj * cap + tab[jj, 16 + 2 * g + s // 16])
                 o[dst, :] = ov[tile(t0 + k), :]
                 gr[dst, :] = gv[tile(t0 + k), :]
                 return 0
@@ -629,7 +629,7 @@
             g = (d + k) % 8
             for m in range(2):
                 s = origin(g, m, j)
-                at = tab[16 + j, 2 * g + m]
+                at = tab[j, 16 + 2 * g + m]
                 got = fin[a, jnp.maximum(at, 0)].astype(F32)
                 ex[a, k, m] = jnp.where(at >= 0, got, 0.0).astype(BF)
                 done.append(deliver(me, ex.at[a, k, m], rec.at[a, d, s % 2],
@@ -687,15 +687,14 @@
     c0 = jnp.zeros((16, 16), jnp.int32)
     c1 = jnp.zeros((16, 16), jnp.int32)
     for k in range(GROUPS):
-        c0 = jnp.where(g == k, cnt[k, 0], c0)
-        c1 = jnp.where(g == k, cnt[k, 1], c1)
+        c0 = jnp.where(g == k, cnt[0, k], c0)
+        c1 = jnp.where(g == k, cnt[1, k], c1)
     s1 = (c0 + 127) // 128 * 8
     left0 = jnp.clip(c0 - T * s, 0, T)
     left1 = jnp.where(s >= s1, jnp.clip(c1 - T * (s - s1), 0, T), 0)
     live = left0 + left1 > 0
     one = f(i32(live))
-    mm = lambda a, b, dims: lax.dot_general(a, b, (dims, ((), ())), preferred_element_type=F32,
-                                            precision=lax.Precision.HIGHEST)
+    mm = lambda a, b, dims: lax.dot_general(a, b, (dims, ((), ())), preferred_element_type=F32)
     rank = mm(one, f(i32(j < q)), ((1,), (0,)))
     place = jnp.where(live, i32(rank), -1)
     orders = jnp.zeros((16, 16), jnp.int32)
@@ -709,10 +708,10 @@
         rows1 = jnp.where(q == k, i32(pick(left1)), rows1)
     out[...] = jnp.zeros_like(out)
     out[0:16, 0:16] = orders
-    out[16:32, 0:16] = place
+    out[0:16, 16:32] = place
     nrow = mm(jnp.ones((8, 16), F32), one, ((1,), (1,)))[0:1, :]
     ok = []
-    base = 32
+    col0 = 32
     for cap, chunks in plans:
         fits = jnp.max(nrow) <= cap
         for lo, hi, r in chunks:
@@ -729,36 +728,26 @@
             used = jnp.sum(hot, axis=1, keepdims=True)
             col = f(i32(f(qq) == at + float(lo)))
             sel = lambda v: jnp.sum(col * mm(hot, f(v), ((1,), (0,))), axis=1, keepdims=True) * used
-            out[base:base + nt, 0:1] = i32(dev * float(hi - lo) + at)
-            out[base:base + nt, 1:2] = i32(sel(rows0))
-            out[base:base + nt, 2:3] = i32(sel(rows1))
+            for i, v in enumerate((dev * float(hi - lo) + at, sel(rows0), sel(rows1))):
+                out[0:nt, col0 + i:col0 + i + 1] = i32(v)
             ncol = jnp.clip(jnp.sum(one, axis=1, keepdims=True) - lo, 0.0, float(hi - lo))
             ocol = mm(f(i32(q < j)), jnp.broadcast_to(ncol, (16, 8)), ((1,), (0,)))[:, 0:1]
             back = jnp.clip(i32(ocol) + q - lo, 0, nt - 1)
-            out[base + nt:base + nt + 16, 0:16] = back + jnp.where(rows1 > 0, nt, 0)
-            base += nt + 16
+            out[0:16, col0 + 4:col0 + 20] = back + jnp.where(rows1 > 0, nt, 0)
+            col0 += 20
             fits = jnp.logical_and(fits, jnp.sum(n) <= nt)
         ok.append(fits)
     level = jnp.int32(len(plans))
     for i in range(len(plans) - 1, -1, -1):
         level = jnp.where(ok[i], i, level)
-    lane = lax.broadcasted_iota(jnp.int32, (8, 16), 1)
-    out[base:base + 8, 0:16] = jnp.where(lane == 0, level, 0)
-
-
-def table_base(plans, index):
-    base = 32
-    for cap, chunks in plans[:index]:
-        for lo, hi, r in chunks:
-            base += r // T + 16
-    return base
+    lane = lax.broadcasted_iota(jnp.int32, (8, 128), 1)
+    out[0:8, :] = jnp.where(lane == 127, level, out[0:8, :])
 
 
 def plan_table(plans, counts):
-    rows = table_base(plans, len(plans)) + 8
     return pl.pallas_call(
         functools.partial(plan_kernel, plans),
-        out_shape=jax.ShapeDtypeStruct((rows, 16), jnp.int32),
+        out_shape=jax.ShapeDtypeStruct((64, 128), jnp.int32),
         in_specs=[pl.BlockSpec(memory_space=pltpu.SMEM)],
         out_specs=pl.BlockSpec(memory_space=pltpu.VMEM),
         name="tile_plan",
@@ -780,17 +769,14 @@
      asend, arecv, bsend, brecv, qsend, qrecv) = rest[nch * len(names):]
     up, down = {"dp": (z + 1) % 4 * 2 + c}, {"dp": (z + 3) % 4 * 2 + c}
     mate = {"dp": z * 2 + 1 - c}
-    owners = [((d + k) % 8, spot(d, 2 * j + hh)) for k in range(8) for hh in range(2)]
     senders = [((d + 8 - k) % 8, origin((d + 8 - k) % 8, m, j) // 2) for k in range(8) for m in range(2)]
     greet([plane("x", x + 1, j), plane("x", x + 3, j), plane("y", y + 1, j), plane("y", y + 3, j),
-           up, down, mate], owners + senders)
+           up, down, mate], senders)
     finish = []
     rb = (rb0, rb1)
     offs = []
-    b = base
-    for lo, hi, r in chunks:
-        offs.append(b)
-        b += r // T + 16
+    for i in range(nch):
+        offs.append(base + 20 * i)
     first_row = [sum(r for _, _, r in chunks[:i]) for i in range(nch)]
 
     def remote(src, dst, ssem, rsem, dev):
@@ -906,11 +892,11 @@
         r0 = first_row[ch]
 
         def pack(t, _):
-            src = tab[offs[ch] + t, 0]
+            src = tab[t, offs[ch]]
             xt, st = xg[src].astype(F32), sg[src].astype(F32)
             dst = tile(r0 // T + t)
             for e in range(2):
-                keep = iota < tab[offs[ch] + t, 1 + e]
+                keep = iota < tab[t, offs[ch] + 1 + e]
                 cs = slice(e * DS, (e + 1) * DS)
                 xcat[dst, cs] = jnp.where(keep, xt, 0.0).astype(BF)
                 scat[dst, cs] = jnp.where(keep, st, 0.0).astype(BF)
@@ -1052,7 +1038,7 @@
 
         def unpack(jj, _):
             for i in range(nt):
-                src = tab[offs[ch] + r // T + jj, lo + i]
+                src = tab[jj, offs[ch] + 4 + lo + i]
                 ob[jj, i] = ov[src]
                 gb[jj, i] = gv[src]
             return 0
@@ -1165,28 +1151,34 @@
     drain(gather(0))
     first(0)
     if nch == 2:
-        za, gb_ = exchange_chunk(0), gather(1)
-        step(za)
-        more = True
-        while step(za):
-            more = more and step(gb_, 2)
-        drain(gb_)
+        za, nx = exchange_chunk(0), gather(1)
+        for n in (1, 3, 3, 0):
+            step(za)
+            step(nx, n)
+        drain(nx)
         first(1)
         zb = exchange_chunk(1)
         step(zb)
+        step(za)
+        step(za)
+        step(zb)
+        drain(za)
         second(0)
         ra = reduce_chunk(0)
         step(ra)
-        while step(zb):
-            step(ra)
-        drain(ra)
+        for n in (1, 2, 1, 2):
+            step(zb)
+            step(ra, n)
+        drain(zb)
         second(1)
         rl = reduce_chunk(1)
+        step(rl)
+        drain(ra)
     else:
         drain(exchange_chunk(0))
         second(0)
         rl = reduce_chunk(0)
-    step(rl)
+        step(rl)
     weight_grads()
     drain(rl)
 
@@ -1195,7 +1187,7 @@
             g = (d + k) % 8
             for m in range(2):
                 s = origin(g, m, j)
-                at = tab[16 + j, 2 * g + m]
+                at = tab[j, 16 + 2 * g + m]
                 got = fin[a, jnp.maximum(at, 0)].astype(F32)
                 ex[a, k, m] = jnp.where(at >= 0, got, 0.0).astype(BF)
                 finish.append(deliver(me, ex.at[a, k, m], rec.at[a, d, s % 2],
@@ -1248,7 +1240,7 @@
                 dma(2, 8, 2), dma(2, 8, 2)]
     w = s((2, HID, DS), BF)
     return pl.pallas_call(
-        functools.partial(layer_kernel, cap, chunks, table_base(plans, index)),
+        functools.partial(layer_kernel, cap, chunks, 32 + 20 * sum(len(ch) for _, ch in plans[:index])),
         out_shape=(s((OWN, DM), BF), s((1, OWN), F32), s((OWN, DM), BF), w, w, w),
         in_specs=[pl.BlockSpec(memory_space=pltpu.SMEM), vm, vm, vm, any_, any_, any_],
         out_specs=(vm,) * 6,
@@ -1273,15 +1265,16 @@
 def per_device(routed_rows, out_cotangent, route_weight, expert_counts, w_gate, w_up, w_down):
     rw = route_weight.reshape(1, OWN)
     wg, wu = jnp.swapaxes(w_gate, 1, 2), jnp.swapaxes(w_up, 1, 2)
-    tab = plan_table(PLANS, expert_counts)
-    pick = tab[table_base(PLANS, len(PLANS)), 0]
+    counts = expert_counts.T
+    tab = plan_table(PLANS, counts)
+    pick = tab[0, 127]
 
     def fast(i, rows, oc, rw, counts, tab, wg, wu, wd):
         return layer(PLANS, i, 3 + i, tab, rows, oc, rw, wg, wu, wd)
 
     branches = [functools.partial(fast, i) for i in range(len(PLANS))] + [run]
     layer_out, grad_weight, grad_rows, dg, du, dd = lax.switch(
-        pick, branches, routed_rows, out_cotangent, rw, expert_counts, tab, wg, wu, w_down)
+        pick, branches, routed_rows, out_cotangent, rw, counts, tab, wg, wu, w_down)
     return (layer_out, grad_weight.reshape(OWN), grad_rows,
             jnp.swapaxes(dg, 1, 2), jnp.swapaxes(du, 1, 2), dd)
 

time: 155 us -> 142 us (0.916)
  Pallas kernels: 145 us -> 132 us
    pallas_call x1, Pallas kernels: 143 us -> 130 us  [layer(): pl.pallas_call(functools.partial(layer_kernel, cap, chunks, 32 + 20 * sum...]
    unnamed x7 -> x6, local copies, waits for them, and re-layouts: 7 us -> 5.65 us
where the time goes in v4:
time: 142 us; the launch traced here: 140 us
  Pallas kernels  132 us (93%)
  local copies, waits for them, and re-layouts  6.24 us (4%)
    pallas_call x1, Pallas kernels, layer(): pl.pallas_call(functools.partial(layer_kernel, cap, chunks, 32 + 20 * sum...  130 us
    unnamed x6, local copies, waits for them, and re-layouts  5.65 us

profile of v4, /device:TPU:1, one launch (start us, length us, event | category | flops | bytes accessed | tf_op | source)
XLA Modules:
  0.0 139.7 jit_solution(426516486666125903)
XLA Ops:
  0.6 1.7 %tile_plan.1 = s32[64,128]{1,0:T(8,128)S(1)} custom-call(s32[2,8]{1,0:T(2,128)} %bitcast.27), custom_call_target="tpu_custom_call" | custom-call | tf_op jit(solution)/shard_map/tile_plan/pallas_call | solution.py:748
  2.3 0.6 slice.4
  3.6 130.4 %conditional.1 = (bf16[32,4096]{1,0:T(8,128)(2,1)S(1)}, bf16[32,4096]{1,0:T(8,128)(2,1)}, bf16[2,448,512]{2,1,0:T(8,128)(2,1)S(1)}, bf16[2,448,512]{2,1,0:T(8,12...) conditional(s32[]{:T(128)} %bitcast.10, (f32[32]{0:T(128)}, ...), branch_computations={%region_0.0_spmd, %region_1.0_spmd, %region_2.0_spmd} | conditional | bytes 1049452 | solution.py:1276
  3.6 130.2 %layer_8_1536.1 = (bf16[32,4096]{1,0:T(8,128)(2,1)S(1)}, f32[1,32]{1,0:T(1,128)S(1)}, bf16[32,4096]{1,0:T(8,128)(2,1)}, bf16[2,448,512]{2,1,0:T(8,128)(2,1)S(1)}...) custom-call(s32[64,128]{1,0:T(8,128)S(1)} %get-tuple-element.59.tab, ...), custom_call_target="tpu_custom_call" | custom-call | tf_op jit(solution)/shard_map/cond/branch_0_fun/layer_8_1536/pallas_call | solution.py:1242
  134.0 0.7 copy.41
  134.7 0.5 copy.42
  135.2 1.7 %copy.43 = bf16[32,4096]{1,0:T(8,128)(2,1)} copy(bf16[32,4096]{1,0:T(8,128)(2,1)} %get-tuple-element.150) | data formatting | bytes 524288
  136.9 0.9 copy.44
  137.8 0.9 copy.45
  138.7 0.9 copy.46
